TPU v7x, 512 devices: a whole 4x8x8 slice. The times are simulated.
512 devices in a mesh: seq: 128 (over z, y_lo, x), ch: 4 (over y_hi, core).
Axes of the slice: x: 4, y: 8 (y_hi: 2, y_lo: 4; y = y_hi * 4 + y_lo), z: 8, core: 2. Of those that a mesh axis runs over, the one named last changes fastest.
Arguments:
- inputs: float32 [768, 32768], P('ch', 'seq'), may hold values from -24 to 24
- weight: bfloat16 [3, 768, 768], P(None, 'ch'), may hold values from -0.125 to 0.125
- grad_out: float32 [768, 32768], P('ch', 'seq'), may hold values from -6 to 6
Outputs:
- outputs: float32 [768, 32768], P('ch', 'seq')
- grad_inputs: float32 [768, 32768], P('ch', 'seq')
- grad_weight: float32 [3, 768, 768], P(None, 'seq', 'ch')
All inputs are finite; a program needn't handle non-finite values.
Results may differ from a plain program's by a relative error of at most 0.0047.
Values may be sent and summed in bfloat16 or wider, within the bound.
A program may use at most 64 MiB of HBM per device.

v0:
```python
import math

import jax
import jax.numpy as jnp
from jax import lax
from jax.sharding import PartitionSpec as P


def from_behind(value, axis, steps):
    count = lax.axis_size(axis)
    initial, last = (max(0, -steps), min(count, count - steps))
    return lax.ppermute(value, axis, [(source, source + steps) for source in range(initial, last)])


def gelu_parts(value):
    cdf = 0.5 * (1.0 + jax.scipy.special.erf(value * (1.0 / math.sqrt(2.0))))
    pdf = jnp.exp(-0.5 * value * value) * (1.0 / math.sqrt(2.0 * math.pi))
    return (value * cdf, cdf + value * pdf)


def back_proj(kernel, grad_cols):
    return lax.dot_general(
        kernel, grad_cols, (((0,), (0,)), ((), ())), preferred_element_type=jnp.float32
    )


def cols_inner(left_cols, grad_cols):
    return lax.dot_general(
        left_cols, grad_cols, (((1,), (1,)), ((), ())), preferred_element_type=jnp.float32
    )


def shards(inputs, weight, grad_out):
    seq_count = lax.axis_size("seq")
    reach = min(8, seq_count // 2)
    lowered = inputs.astype(jnp.bfloat16)
    whole = lax.all_gather(lowered, "ch", axis=0, tiled=True)
    before = from_behind(whole, "seq", reach)
    after = from_behind(whole, "seq", -reach)
    preact = jnp.dot(weight[1], whole, preferred_element_type=jnp.float32)
    preact = preact + jnp.dot(weight[0], before, preferred_element_type=jnp.float32)
    preact = preact + jnp.dot(weight[2], after, preferred_element_type=jnp.float32)
    act, deriv = gelu_parts(preact)
    outputs = inputs + act
    delta = (grad_out * deriv).astype(jnp.bfloat16)
    delta_after = from_behind(delta, "seq", -reach)
    delta_before = from_behind(delta, "seq", reach)
    partial_value = back_proj(weight[1], delta)
    partial_value = partial_value + back_proj(weight[0], delta_after)
    partial_value = partial_value + back_proj(weight[2], delta_before)
    summed = lax.psum_scatter(
        partial_value.astype(jnp.bfloat16), "ch", scatter_dimension=0, tiled=True
    ).astype(jnp.float32)
    grad_inputs = grad_out + summed
    term = jnp.stack(
        [cols_inner(before, delta), cols_inner(whole, delta), cols_inner(after, delta)]
    )
    scale = (inputs.shape[1] * seq_count) ** (-0.5)
    grad_weight = lax.psum_scatter(term, "seq", scatter_dimension=1, tiled=True) * scale
    return (outputs, grad_inputs, grad_weight)


def solution(mesh):
    return jax.shard_map(
        shards,
        mesh=mesh,
        in_specs=(P("ch", "seq"), P(None, "ch", None), P("ch", "seq")),
        out_specs=(P("ch", "seq"), P("ch", "seq"), P(None, "seq", "ch")),
        check_vma=False,
    )
```

profile of v0, /device:TPU:32, one launch (start us, length us, event | category | flops | bytes accessed | tf_op | source)
XLA Modules:
  0.0 1524.5 jit_solution(18167517413423075984)
XLA Ops:
  8.0 0.0 copy-start.2
  8.0 0.0 copy-start
  8.0 0.0 copy-start.1
  8.0 0.0 reduce-scatter.4.cloned.1.call-start
  8.1 1.0 convert_element_type.15
  9.1 11.9 all_gather.3
  21.0 2.1 collective-permute-start
  23.1 1.3 collective-permute-start.1
  24.4 1.2 fusion.8
  25.6 6.4 collective-permute-done
  32.0 0.0 copy-done
  32.0 0.2 convolution_add_fusion.3
  32.3 28.5 %collective-permute-done.1 = bf16[768,256]{1,0:T(8,128)(2,1)S(1)} collective-permute-done((bf16[768,256]{1,0:T(8,128)(2,1)S(1)}, bf16[768,256]{1,0:T(8,128)(2,1)S(1)}, u32[]{:S(2)}, u32[]{:S(2)}) %collective-permute-start.1) | collective-permute-done | bytes 393248 | tf_op jit(solution)/shard_map/ppermute | solution.py:12
  60.7 0.0 copy-done.2
  60.7 0.0 copy-done.1
  60.7 1.0 fusion.21
  61.8 1.3 collective-permute-start.2
  63.0 0.3 fusion.6
  63.3 5.5 collective-permute-start.3
  68.8 1.9 collective-permute-done.2
  70.7 0.3 convolution_add_fusion.1
  71.0 0.0 collective-permute-done.3
  71.0 0.3 fusion.1
  71.3 0.9 copy.13
  72.2 0.0 reduce-scatter.4.cloned.1.call-update
  72.3 0.0 all-reduce.3.cloned.1.call-start
  72.3 0.3 convolution_bitcast_fusion.1
  72.6 0.3 convolution_bitcast_fusion
  72.9 0.3 convolution_bitcast_fusion.2
  73.2 0.1 pad_maximum_fusion
  73.3 2.8 copy.10
  76.1 0.0 all-reduce.3.cloned.1.call-update
  76.1 0.1 copy.9
  76.3 1.3 dynamic-slice
  78.2 39.1 %reduce-scatter.4.cloned.1.call-done = bf16[192,256]{1,0:T(8,128)(2,1)} async-done(((bf16[768,256]{1,0:T(8,128)(2,1)}), bf16[192,256]{1,0:T(8,128)(2,1)}) %reduce-scatter.4.cloned.1.call-update) | async-done | bytes 98320
  117.3 1.0 copy.14
  118.4 0.8 copy.11
  119.2 1396.5 %all-reduce.3.cloned.1.call-done = f32[3,768,192]{2,0,1:T(4,128)} async-done(((f32[3,768,192]{2,0,1:T(4,128)}), f32[3,768,192]{2,0,1:T(4,128)}) %all-reduce.3.cloned.1.call-update) | async-done | bytes 1769488
  1515.7 0.7 dynamic-slice_multiply_fusion
  1516.5 0.6 copy.12
  (1 shorter events, 0.0 us)
Async XLA Ops:
  8.0 52.7 %copy-start.2 = (f32[192,256]{1,0:T(8,128)S(1)}, f32[192,256]{1,0:T(8,128)}, u32[]{:S(2)}) copy-start(f32[192,256]{1,0:T(8,128)} %param.3) | copy-start | bytes 589828
  8.0 24.0 %copy-start = (bf16[3,192,768]{2,1,0:T(8,128)(2,1)S(1)}, bf16[3,192,768]{2,1,0:T(8,128)(2,1)}, u32[]{:S(2)}) copy-start(bf16[3,192,768]{2,1,0:T(8,128)(2,1)} %param.4) | copy-start | bytes 2654212
  8.0 52.7 %copy-start.1 = (f32[192,256]{1,0:T(8,128)S(1)}, f32[192,256]{1,0:T(8,128)}, u32[]{:S(2)}) copy-start(f32[192,256]{1,0:T(8,128)} %param.5) | copy-start | bytes 589828
  8.0 109.3 %reduce-scatter.4.cloned.1.call-start = ((), (), s32[]{:S(2)}) async-start(), calls=%async_computation.1 | async-start | bytes 491520
  21.0 11.0 collective-permute-start
  23.1 37.6 %collective-permute-start.1 = (bf16[768,256]{1,0:T(8,128)(2,1)S(1)}, bf16[768,256]{1,0:T(8,128)(2,1)S(1)}, u32[]{:S(2)}, u32[]{:S(2)}) collective-permute-start(bf16[768,256]{1,0:T(8,128)(2,1)S(1)} %all_gather.3), channel_id=1, source_target_pairs={{32,0},{36,4},{40,8},{44,12},{48,16},{52,20},{56,24},{60,28},{64,3... | collective-permute-start | bytes 1179656 | tf_op jit(solution)/shard_map/ppermute | solution.py:12
  61.8 9.0 collective-permute-start.2
  63.3 7.7 collective-permute-start.3
  72.3 1443.5 %all-reduce.3.cloned.1.call-start = ((), (), s32[]{:S(2)}) async-start(), calls=%async_computation.2 | async-start | bytes 6291456
Sparse Core Ops, SparseCore 0:
  72.4 44.9 reduce-scatter.3
Sparse Core Ops, SparseCore 1:
  76.2 1439.4 all-reduce.2
where the time goes:
time: 1520 us
  waiting for transfers between devices  1470 us (97%)
  between operations  16.3 us (1%)
    unnamed x4, waiting for transfers between devices  1440 us
    ppermute x4, waiting for transfers between devices, from_behind(): lax.ppermute(value, axis, [(source, source + steps) for source in range(i...  36.8 us
  transfers between devices with their start and end apart: 6, of which 5 were waited for; matrix products, arithmetic and copies ran while one was open for 1% of the time, Pallas kernels for 0%

commit v1 on v0

v1 whole, which is shorter than its diff:
```python
import math

import jax
import jax.numpy as jnp
from jax import lax
from jax.experimental import pallas as pl
from jax.experimental.pallas import tpu as pltpu
from jax.sharding import PartitionSpec as P

MESH = pl.DeviceIdType.MESH
F32, BF16 = jnp.float32, jnp.bfloat16
GROUP = 192
HALF = GROUP // 2
COLS = 256
LANES = 640

NAMES = []
for k in range(2):
    NAMES += [f"{n}{k}" for n in ("own", "up", "dn", "zu", "zd", "cup", "cdn", "czu", "czd", "cr", "dy", "dz")]
NAMES += ["rup", "rdn", "rs0", "rs1", "fa", "fb", "ga", "gb"]
NAMES += ["x1a", "x1b", "x2a", "x2b", "x2c", "x2d"]
NAMES += [f"y{d}" for d in range(1, 4)] + [f"z{d}" for d in range(1, 8)]
SLOT = {name: i for i, name in enumerate(NAMES)}


def dot(a, b, ca, cb):
    return lax.dot_general(a, b, (((ca,), (cb,)), ((), ())), preferred_element_type=F32)


def one_hot(hit):
    return jnp.where(hit, 1.0, 0.0).astype(BF16)


def kernel(
    scale, x_ref, w_ref, g_ref, out_ref, gin_ref, gw_ref,
    xb, wp, db, ds, ps, pown, xr1, xs2, xr2, ys, yr, zs, zr, rf, rb, rs1r, rs2s, rel, rs2r, send, recv,
):
    s, ch = lax.axis_index("seq"), lax.axis_index("ch")
    z, yl, x = lax.div(s, 16), lax.rem(lax.div(s, 4), 4), lax.rem(s, 4)
    yh, c = lax.div(ch, 2), lax.rem(ch, 2)
    y = yh * 4 + yl
    late = lax.div(yl, 2)

    def at(z, y, x, c):
        z, y, x = lax.rem(z, 8), lax.rem(y, 8), lax.rem(x, 4)
        return (z * 16 + lax.rem(y, 4) * 4 + x, lax.div(y, 4) * 2 + c)

    def ch_of(y):
        return lax.div(lax.rem(y, 8), 4) * 2 + c

    core = at(z, y, x, 1 - c)
    y_up, y_dn = at(z, y + 2, x, c), at(z, y + 6, x, c)
    x_up, x_dn = at(z, y, x + 1, c), at(z, y, x + 3, c)
    y_in = at(z, yh * 4 + lax.rem(yl + 2, 4), x, c)
    z_to = at(z + 1 + 6 * late, y, x, c)
    y_of = [None] + [at(z, yh * 4 + lax.rem(yl + d, 4), x, c) for d in range(1, 4)]
    z_of = [None] + [at(z + d, y, x, c) for d in range(1, 8)]

    barrier = pltpu.get_barrier_semaphore()
    peers = [core, y_up, y_dn, x_up, x_dn] + y_of[1:] + z_of[1:]
    for peer in peers:
        pl.semaphore_signal(barrier, inc=1, device_id=peer, device_id_type=MESH)

    live = {}

    def go(name, src, dst, to):
        i = SLOT[name]
        live[name] = pltpu.make_async_remote_copy(
            src_ref=src, dst_ref=dst, send_sem=send.at[i], recv_sem=recv.at[i], device_id=to, device_id_type=MESH
        )
        live[name].start()

    def got(name):
        live[name].wait_recv()

    row = lax.broadcasted_iota(jnp.int32, (384, 384), 0)
    col = lax.broadcasted_iota(jnp.int32, (384, 384), 1)
    upper = jnp.where(row >= GROUP, 1, 0)
    r = row - GROUP * upper
    six = lax.shift_right_logical(r * 10923, 16)
    source = (six & 1) * 96 + (lax.shift_right_logical(six, 1) & 3) * 24 + lax.shift_right_logical(six, 3) * 6 + r - six * 6
    order = one_hot(source + GROUP * upper == col)
    lowered = x_ref[...].astype(BF16)
    xb[1, ch] = dot(order[:GROUP, :GROUP], lowered, 1, 0).astype(BF16)

    pl.semaphore_wait(barrier, len(peers))

    t_to = 2 * late
    t_in = 2 - 2 * late
    part = [pl.ds(HALF * k, HALF) for k in range(2)]
    ch_dn, ch_up, ch_far = ch_of(y + 6), ch_of(y + 2), ch_of(y + 4)
    for k in range(2):
        mine = xb.at[1, ch, part[k]]
        go(f"up{k}", mine, xb.at[t_to, ch, part[k]], y_up)
        go(f"dn{k}", mine, xb.at[t_to, ch, part[k]], y_dn)
        go(f"own{k}", mine, mine, core)

    for t in range(3):
        for b in range(2):
            cols = slice(384 * b, 384 * (b + 1))
            wp[t, :, cols] = dot(w_ref[t, :, cols], order, 1, 1).astype(BF16)

    for k in range(2):
        got(f"up{k}")
        block = xb.at[t_in, ch_dn, part[k]]
        if k == 0:
            go("rup", block, xb.at[1, ch_dn, part[k]], y_up)
        go(f"zu{k}", block, xb.at[t_to, ch_dn, part[k]], z_to)
        go(f"cup{k}", block, block, core)
        got(f"dn{k}")
        block = xb.at[t_in, ch_up, part[k]]
        if k == 1:
            go("rdn", block, xb.at[1, ch_up, part[k]], y_dn)
        go(f"zd{k}", block, xb.at[t_to, ch_up, part[k]], z_to)
        go(f"cdn{k}", block, block, core)
    for k in range(2):
        got(f"zu{k}")
        block = xb.at[t_to, ch_dn, part[k]]
        go(f"czu{k}", block, block, core)
        got(f"zd{k}")
        block = xb.at[t_to, ch_up, part[k]]
        go(f"czd{k}", block, block, core)
    for k in range(2):
        got(("rup", "rdn")[k])
        block = xb.at[1, ch_far, part[k]]
        go(f"cr{k}", block, block, core)
    for k in range(2):
        for name in ("own", "cup", "cdn", "czu", "czd", "cr"):
            got(f"{name}{k}")

    first = jnp.where(s < 8, 0.0, 1.0).astype(F32)
    last = jnp.where(s >= 120, 0.0, 1.0).astype(F32)
    preact = dot(wp[1], xb[1].reshape(768, COLS), 1, 0)
    preact += dot(wp[0], xb[0].reshape(768, COLS), 1, 0) * first
    preact += dot(wp[2], xb[2].reshape(768, COLS), 1, 0) * last
    cdf = 0.5 * (1.0 + lax.erf(preact * (1.0 / math.sqrt(2.0))))
    pdf = jnp.exp(-0.5 * preact * preact) * (1.0 / math.sqrt(2.0 * math.pi))
    delta32 = g_ref[...] * (cdf + preact * pdf)
    delta = delta32.astype(BF16)
    db[1] = delta

    for k in range(2):
        go(f"dy{k}", db.at[1, part[k]], db.at[t_to, part[k]], y_in)
    out_ref[...] = x_ref[...] + preact * cdf

    zero = jnp.zeros((64, COLS), BF16)
    ds[0:192] = (delta32 * first).astype(BF16)
    ds[192:256] = zero
    ds[256:320] = zero
    ds[320:384] = zero
    ds[384:448] = zero
    ds[448:640] = delta
    ds[640:832] = (delta32 * last).astype(BF16)
    ds[832:896] = zero

    def chunk(step):
        rows = pl.ds(pl.multiple_of(lax.rem(x + step, 4) * 48, 48), 48)
        before, here, after = [xb[t, :, rows, :].reshape(GROUP, COLS) for t in range(3)]
        left = dot(before, ds[0:256], 1, 1) + dot(here, ds[256:512], 1, 1)
        return left, dot(here, ds[512:640], 1, 1), dot(after, ds[640:896], 1, 1)

    def keep(ref, parts, kind):
        ref[:, 0:256] = parts[0].astype(kind)
        ref[:, 256:384] = parts[1].astype(kind)
        ref[:, 384:640] = parts[2].astype(kind)

    keep(ps.at[2], chunk(2), BF16)
    go("x1a", ps.at[2, part[0]], xr1.at[0], x_up)
    go("x1b", ps.at[2, part[1]], xr1.at[1], x_dn)
    keep(ps.at[1], chunk(1), BF16)
    go("x2b", ps.at[1, part[1]], xr2.at[1], x_up)
    keep(ps.at[3], chunk(3), BF16)
    go("x2c", ps.at[3, part[0]], xr2.at[2], x_dn)
    keep(pown, chunk(0), F32)

    for k in range(2):
        got(f"dy{k}")
        go(f"dz{k}", db.at[t_in, part[k]], db.at[t_to, part[k]], z_to)

    got("x1a")
    xs2[0] = (xr1[0].astype(F32) + ps[1, 0:HALF].astype(F32)).astype(BF16)
    go("x2a", xs2.at[0], xr2.at[0], x_up)
    got("x1b")
    xs2[1] = (xr1[1].astype(F32) + ps[3, HALF:GROUP].astype(F32)).astype(BF16)
    go("x2d", xs2.at[1], xr2.at[3], x_dn)

    for k in range(2):
        got(f"dz{k}")
    for q in range(4):
        cols = slice(GROUP * q, GROUP * (q + 1))
        back = dot(w_ref[1, :, cols], db[1], 0, 0)
        back += dot(w_ref[0, :, cols], db[2], 0, 0) * last
        back += dot(w_ref[2, :, cols], db[0], 0, 0) * first
        rf[q] = back
        rb[q] = back.astype(BF16)
    for h in range(2):
        go(f"rs{h}", rb.at[h * 2 + 1 - c], rs1r.at[h], core)
    for h in range(2):
        got(f"rs{h}")
    rs2s[...] = (rf[(1 - yh) * 2 + c] + rs1r[1 - yh].astype(F32)).astype(BF16)
    go("fa", rs2s.at[part[0]], rel.at[0], y_up)
    go("fb", rs2s.at[part[1]], rel.at[1], y_dn)

    for name in ("x2a", "x2b", "x2c", "x2d"):
        got(name)
    got("fa")
    go("ga", rel.at[0], rs2r.at[part[0]], y_up)
    got("fb")
    go("gb", rel.at[1], rs2r.at[part[1]], y_dn)
    top = pown[0:HALF] + xr2[0].astype(F32) + xr2[2].astype(F32)
    low = pown[HALF:GROUP] + xr2[1].astype(F32) + xr2[3].astype(F32)
    row = lax.broadcasted_iota(jnp.int32, (GROUP, GROUP), 0)
    col = lax.broadcasted_iota(jnp.int32, (GROUP, GROUP), 1)
    twelve = lax.shift_right_logical(row * 5462, 16)
    turn = one_hot((twelve & 3) * 48 + lax.shift_right_logical(twelve, 2) * 12 + row - twelve * 12 == col)
    turned = dot(turn[:, :HALF], top.astype(BF16), 1, 0) + dot(turn[:, HALF:], low.astype(BF16), 1, 0)
    ys[...] = turned.astype(BF16).reshape(4, 48, LANES)
    for d in (2, 1, 3):
        go(f"y{d}", ys.at[lax.rem(yl + d, 4)], yr.at[d - 1], y_of[d])
    total = ys[yl].astype(F32)
    for d in (1, 3, 2):
        got(f"y{d}")
        total += yr[d - 1].astype(F32)

    row = lax.broadcasted_iota(jnp.int32, (64, 48), 0)
    col = lax.broadcasted_iota(jnp.int32, (64, 48), 1)
    inner = row & 7
    spread = one_hot((lax.shift_right_logical(row, 3) * 6 + inner == col) & (inner < 6))
    zs[...] = dot(spread, total.astype(BF16), 1, 0).astype(BF16).reshape(8, 8, LANES)
    for d in (4, 3, 5, 2, 6, 1, 7):
        go(f"z{d}", zs.at[lax.rem(z + d, 8)], zr.at[d - 1], z_of[d])

    got("ga")
    got("gb")
    gin_ref[...] = g_ref[...] + (rf[yh * 2 + c] + rs1r[yh].astype(F32) + rs2r[...].astype(F32))

    total = zs[z].astype(F32)
    for d in (1, 7, 2, 6, 3, 5, 4):
        got(f"z{d}")
        total += zr[d - 1].astype(F32)
    total = total * scale
    for t in range(3):
        gw_ref[t] = total[0:6, GROUP * t : GROUP * (t + 1)]

    for name in NAMES:
        live[name].wait_send()


def shards(inputs, weight, grad_out):
    scale = (inputs.shape[1] * lax.axis_size("seq")) ** (-0.5)
    vmem = pl.BlockSpec(memory_space=pltpu.VMEM)
    count = len(NAMES)

    def body(*refs):
        kernel(scale, *refs)

    return pl.pallas_call(
        body,
        out_shape=(
            jax.ShapeDtypeStruct((GROUP, COLS), F32),
            jax.ShapeDtypeStruct((GROUP, COLS), F32),
            jax.ShapeDtypeStruct((3, 6, GROUP), F32),
        ),
        in_specs=[vmem] * 3,
        out_specs=(vmem,) * 3,
        scratch_shapes=[
            pltpu.VMEM((3, 4, GROUP, COLS), BF16),
            pltpu.VMEM((3, GROUP, 768), BF16),
            pltpu.VMEM((3, GROUP, COLS), BF16),
            pltpu.VMEM((896, COLS), BF16),
            pltpu.VMEM((4, GROUP, LANES), BF16),
            pltpu.VMEM((GROUP, LANES), F32),
            pltpu.VMEM((2, HALF, LANES), BF16),
            pltpu.VMEM((2, HALF, LANES), BF16),
            pltpu.VMEM((4, HALF, LANES), BF16),
            pltpu.VMEM((4, 48, LANES), BF16),
            pltpu.VMEM((3, 48, LANES), BF16),
            pltpu.VMEM((8, 8, LANES), BF16),
            pltpu.VMEM((7, 8, LANES), BF16),
            pltpu.VMEM((4, GROUP, COLS), F32),
            pltpu.VMEM((4, GROUP, COLS), BF16),
            pltpu.VMEM((2, GROUP, COLS), BF16),
            pltpu.VMEM((GROUP, COLS), BF16),
            pltpu.VMEM((2, HALF, COLS), BF16),
            pltpu.VMEM((GROUP, COLS), BF16),
            pltpu.SemaphoreType.DMA((count,)),
            pltpu.SemaphoreType.DMA((count,)),
        ],
        compiler_params=pltpu.CompilerParams(collective_id=0, has_side_effects=True),
    )(inputs, weight, grad_out)


def solution(mesh):
    return jax.shard_map(
        shards,
        mesh=mesh,
        in_specs=(P("ch", "seq"), P(None, "ch", None), P("ch", "seq")),
        out_specs=(P("ch", "seq"), P("ch", "seq"), P(None, "seq", "ch")),
        check_vma=False,
    )
```

time: 1520 us -> 61.8 us (0.04)
  the two profiles are of different devices: /device:TPU:32 before, /device:TPU:10 now
where the time goes in v1:
time: 61.8 us; the launch traced here: 61.6 us
  Pallas kernels  58 us (94%)
  local copies, waits for them, and re-layouts  3 us (5%)
  between operations  0.65 us (1%)
    pallas_call x1, Pallas kernels, shards(): pl.pallas_call(body, out_shape=(jax.ShapeDtypeStruct((GROUP, COLS), F32),...  58 us
    unnamed x7, local copies, waits for them, and re-layouts  3 us

profile of v1, /device:TPU:10, one launch (start us, length us, event | category | flops | bytes accessed | tf_op | source)
XLA Modules:
  0.0 61.6 jit_solution(9925888416198164131)
XLA Ops:
  0.6 58.0 %shard_map.58 = (f32[192,256]{1,0:T(8,128)}, f32[192,256]{1,0:T(8,128)}, f32[3,6,192]{2,1,0:T(8,128)}) custom-call(f32[192,256]{1,0:T(8,128)} %refs_0_.1, bf16[3,192,768]{2,1,0:T(8,128)(2,1)} %refs_1_.1, f32[192,256]{1,0:T(8,128)} %refs_2_.1), custom_call_target="tpu_custom_call" | custom-call | tf_op jit(solution)/shard_map/pallas_call | solution.py:257
  58.6 0.0 copy-start
  58.6 1.7 %copy.9 = f32[192,256]{1,0:T(8,128)} copy(f32[192,256]{1,0:T(8,128)} %get-tuple-element.6) | data formatting | bytes 393216
  60.3 0.0 copy-done
  60.3 0.0 copy-start.1
  60.3 0.7 %copy.10 = f32[192,256]{1,0:T(8,128)} copy(f32[192,256]{1,0:T(8,128)S(1)} %copy-done) | data formatting | bytes 393216
  61.0 0.1 copy-done.1
  61.0 0.6 copy.11
Async XLA Ops:
  58.6 1.7 %copy-start = (f32[192,256]{1,0:T(8,128)S(1)}, f32[192,256]{1,0:T(8,128)}, u32[]{:S(2)}) copy-start(f32[192,256]{1,0:T(8,128)} %get-tuple-element.7) | copy-start | bytes 589828
  60.3 0.7 %copy-start.1 = (f32[3,6,192]{2,1,0:T(8,128)S(1)}, f32[3,6,192]{2,1,0:T(8,128)}, u32[]{:S(2)}) copy-start(f32[3,6,192]{2,1,0:T(8,128)} %get-tuple-element.8) | copy-start | bytes 41476

commit v2 on v0

v2 whole, which is shorter than its diff:
```python
import math

import jax
import jax.numpy as jnp
from jax import lax
from jax.experimental import pallas as pl
from jax.experimental.pallas import tpu as pltpu
from jax.sharding import PartitionSpec as P

MESH = pl.DeviceIdType.MESH
F32, BF16 = jnp.float32, jnp.bfloat16
GROUP = 192
HALF = GROUP // 2
COLS = 256
WIDE = 384
LAST = 256

NAMES = []
for k in range(2):
    NAMES += [f"{n}{k}" for n in ("own", "up", "dn", "zu", "zd", "cup", "cdn", "czu", "czd", "cr", "dy", "dz")]
NAMES += ["rup", "rdn", "near", "far", "away", "co", "cf", "ci", "ct"]
for d in range(1, 4):
    NAMES += [f"{n}{d}" for n in ("so", "sf", "si", "st", "dx", "ya", "yb")]
for d in range(1, 8):
    NAMES += [f"za{d}", f"zb{d}"]
SLOT = {name: i for i, name in enumerate(NAMES)}


def dot(a, b, ca, cb):
    return lax.dot_general(a, b, (((ca,), (cb,)), ((), ())), preferred_element_type=F32)


def one_hot(hit):
    return jnp.where(hit, 1.0, 0.0).astype(BF16)


def grid(rows, cols):
    return [lax.broadcasted_iota(jnp.int32, (rows, cols), axis) for axis in range(2)]


def over(value, factor, bits):
    return lax.shift_right_logical(value * factor, bits)


def kernel(
    x_ref, w_ref, g_ref, act_ref, sum_ref, gw_ref,
    xb, xs, wp, wt, db, dx, dlow, ya, yar, za, zar, zb, zbr, yb, ybr, rf, rb, rr, far_s, far_r, send, recv,
):
    s, ch = lax.axis_index("seq"), lax.axis_index("ch")
    z, yl, x = lax.div(s, 16), lax.rem(lax.div(s, 4), 4), lax.rem(s, 4)
    yh, c = lax.div(ch, 2), lax.rem(ch, 2)
    y = yh * 4 + yl
    late = lax.div(yl, 2)

    def at(z, y, x, c):
        z, y, x = lax.rem(z, 8), lax.rem(y, 8), lax.rem(x, 4)
        return (z * 16 + lax.rem(y, 4) * 4 + x, lax.div(y, 4) * 2 + c)

    core = at(z, y, x, 1 - c)
    y_up, y_dn, y_far = at(z, y + 2, x, c), at(z, y + 6, x, c), at(z, y + 4, x, c)
    y_in = at(z, yh * 4 + lax.rem(yl + 2, 4), x, c)
    z_to = at(z + 1 + 6 * late, y, x, c)
    x_of = [None] + [at(z, y, x + d, c) for d in range(1, 4)]
    y_of = [None] + [at(z, yh * 4 + lax.rem(yl + d, 4), x, c) for d in range(1, 4)]
    z_of = [None] + [at(z + d, y, x, c) for d in range(1, 8)]

    barrier = pltpu.get_barrier_semaphore()
    peers = [core, y_up, y_dn, y_far] + x_of[1:] + y_of[1:] + z_of[1:]
    for peer in peers:
        pl.semaphore_signal(barrier, inc=1, device_id=peer, device_id_type=MESH)

    live = {}

    def go(name, src, dst, to):
        i = SLOT[name]
        live[name] = pltpu.make_async_remote_copy(
            src_ref=src, dst_ref=dst, send_sem=send.at[i], recv_sem=recv.at[i], device_id=to, device_id_type=MESH
        )
        live[name].start()

    def got(*names):
        for name in names:
            live[name].wait_recv()

    row, col = grid(WIDE, WIDE)
    upper = jnp.where(row >= GROUP, 1, 0)
    r = row - GROUP * upper
    six = over(r, 10923, 16)
    source = (six & 1) * 96 + (over(six, 1, 1) & 3) * 24 + over(six, 1, 3) * 6 + r - six * 6
    order = one_hot(source + GROUP * upper == col)
    lowered = x_ref[...].astype(BF16)
    xb[1, yh, c] = dot(order[:GROUP, :GROUP], lowered, 1, 0).astype(BF16)

    pl.semaphore_wait(barrier, len(peers))

    t_to = 2 * late
    t_in = 2 - 2 * late
    part = [pl.ds(HALF * k, HALF) for k in range(2)]
    h_dn, h_up, h_far = lax.div(lax.rem(y + 6, 8), 4), lax.div(lax.rem(y + 2, 8), 4), 1 - yh
    for k in range(2):
        mine = xb.at[1, yh, c, part[k]]
        go(f"up{k}", mine, xb.at[t_to, yh, c, part[k]], y_up)
        mine = xb.at[1, yh, c, part[1 - k]]
        go(f"dn{1 - k}", mine, xb.at[t_to, yh, c, part[1 - k]], y_dn)
    for k in range(2):
        mine = xb.at[1, yh, c, part[k]]
        go(f"own{k}", mine, mine, core)

    def slices(d):
        return pl.ds(pl.multiple_of(lax.rem(x + d, 4) * 48, 48), 48)

    for d in (1, 3, 2):
        go(f"so{d}", xb.at[1, yh, c, slices(d)], xs.at[1, d, yh, c], x_of[d])

    for t in range(3):
        for b in range(2):
            cols = slice(WIDE * b, WIDE * (b + 1))
            wp[t, :, cols] = dot(w_ref[t, :, cols], order, 1, 1).astype(BF16)

    for k in range(2):
        got(f"up{k}")
        block = xb.at[t_in, h_dn, c, part[k]]
        go(f"zu{k}", block, xb.at[t_to, h_dn, c, part[k]], z_to)
        if k == 0:
            go("rup", block, xb.at[1, h_dn, c, part[k]], y_up)
        got(f"dn{1 - k}")
        other = xb.at[t_in, h_up, c, part[1 - k]]
        go(f"zd{1 - k}", other, xb.at[t_to, h_up, c, part[1 - k]], z_to)
        if k == 0:
            go("rdn", other, xb.at[1, h_up, c, part[1 - k]], y_dn)
        go(f"cup{k}", block, block, core)
        go(f"cdn{1 - k}", other, other, core)
    for d in (1, 3, 2):
        go(f"si{d}", xb.at[t_in, :, c, slices(d)], xs.at[t_in, d, :, c], x_of[d])
    wide = w_ref[...]
    for t in range(3):
        wt[t] = wide[t].T.reshape(4, GROUP, GROUP)
    got("so1", "so3", "so2")
    go("co", xs.at[1, 1:4, yh, c], xs.at[1, 1:4, yh, c], core)
    for k in range(2):
        got(f"zu{k}")
        block = xb.at[t_to, h_dn, c, part[k]]
        go(f"czu{k}", block, block, core)
        got(f"zd{1 - k}")
        block = xb.at[t_to, h_up, c, part[1 - k]]
        go(f"czd{1 - k}", block, block, core)
        got(("rup", "rdn")[k])
        block = xb.at[1, h_far, c, part[k]]
        go(f"cr{k}", block, block, core)
    for d in (1, 3, 2):
        go(f"st{d}", xb.at[t_to, :, c, slices(d)], xs.at[t_to, d, :, c], x_of[d])
        go(f"sf{d}", xb.at[1, h_far, c, slices(d)], xs.at[1, d, h_far, c], x_of[d])

    def tap(t):
        return dot(wp[t], xb[t].reshape(768, COLS), 1, 0)

    edge = jnp.where((s < 8) | (s >= 120), 0.0, 1.0).astype(F32)
    for k in range(2):
        got(*[f"{name}{k}" for name in ("own", "cup", "cdn", "cr")])
    preact = tap(1) + tap(t_in)
    got("czu0", "czd1", "czu1", "czd0")
    preact += tap(t_to) * edge
    cdf = 0.5 * (1.0 + lax.erf(preact * (1.0 / math.sqrt(2.0))))
    pdf = jnp.exp(-0.5 * preact * preact) * (1.0 / math.sqrt(2.0 * math.pi))
    delta = (g_ref[...] * (cdf + preact * pdf)).astype(BF16)
    db[1] = delta
    dx[0, 0:GROUP] = delta

    for k in range(2):
        go(f"dy{k}", db.at[1, part[k]], db.at[t_to, part[k]], y_in)
    for d in (1, 3, 2):
        go(f"dx{d}", db.at[1], dx.at[d, 0:GROUP], x_of[d])
    act_ref[...] = preact * cdf
    got("si1", "si3", "si2")
    go("ci", xs.at[t_in, 1:4, :, c], xs.at[t_in, 1:4, :, c], core)
    got("sf1", "sf3", "sf2")
    go("cf", xs.at[1, 1:4, h_far, c], xs.at[1, 1:4, h_far, c], core)
    got("st1", "st3", "st2")
    go("ct", xs.at[t_to, 1:4, :, c], xs.at[t_to, 1:4, :, c], core)

    blocks = [(1 - yh) * 2 + 1 - c, (1 - yh) * 2 + c, yh * 2 + 1 - c, yh * 2 + c]
    for i, q in enumerate(blocks):
        rf[i] = dot(wt[1, q], delta, 1, 0)
    for d in range(4):
        dx[d, GROUP:COLS] = jnp.zeros((COLS - GROUP, COLS), BF16)
        dlow[d, 0:GROUP] = jnp.zeros((GROUP, COLS), BF16)
    for k in range(2):
        got(f"dy{k}")
        go(f"dz{k}", db.at[t_in, part[k]], db.at[t_to, part[k]], z_to)
    for i, q in enumerate(blocks):
        rf[i] += dot(wt[2 - t_in, q], db[t_in], 1, 0)

    first = jnp.where(s < 8, 0.0, 1.0).astype(F32)
    last = jnp.where(s >= 120, 0.0, 1.0).astype(F32)
    own_rows = slices(0)
    got("co", "ci", "cf", "ct")
    sums = None
    for d in (0, 1, 3, 2):
        if d:
            got(f"dx{d}")
        dlow[d, GROUP:COLS] = dx[d, 0:64]
        taps = [(xb[t, :, :, own_rows, :] if d == 0 else xs[t, d]).reshape(GROUP, COLS) for t in range(3)]
        new = [dot(taps[0], dx[d], 1, 1), dot(taps[1], dlow[d], 1, 1), dot(taps[1], dx[d, 64:GROUP], 1, 1), dot(taps[2], dx[d], 1, 1)]
        sums = new if sums is None else [a + b for a, b in zip(sums, new)]

    row, col = grid(GROUP, GROUP)
    twelve = over(row, 5462, 16)
    to_y = one_hot((twelve & 3) * 48 + over(twelve, 1, 2) * 12 + row - twelve * 12 == col)
    six = over(row, 10923, 16)
    at_z = over(six, 1, 2)
    to_z = one_hot(over(at_z, 1, 1) * 48 + (six & 3) * 12 + (at_z & 1) * 6 + row - six * 6 == col)

    zb[...] = dot(to_z, (sums[3] * last).astype(BF16), 1, 0).astype(BF16).reshape(8, 24, LAST)
    for d in (4, 3, 5, 2, 6, 1, 7):
        go(f"zb{d}", zb.at[lax.rem(z + d, 8)], zbr.at[d - 1], z_of[d])
    ya[:, :, 0:256] = dot(to_y, (sums[0] * first + sums[1]).astype(BF16), 1, 0).astype(BF16).reshape(4, 48, 256)
    ya[:, :, 256:WIDE] = dot(to_y, sums[2].astype(BF16), 1, 0).astype(BF16).reshape(4, 48, 128)
    for d in (2, 1, 3):
        go(f"ya{d}", ya.at[lax.rem(yl + d, 4)], yar.at[d - 1], y_of[d])

    got("dz0", "dz1")
    for i, q in enumerate(blocks):
        back = rf[i] + dot(wt[2 - t_to, q], db[t_to], 1, 0) * edge
        if i in (0, 2):
            rb[i // 2] = back.astype(BF16)
            go(("far", "near")[i // 2], rb.at[i // 2], rr.at[i // 2], core)
        else:
            rf[i] = back
    got("far")
    far_s[...] = (rf[1] + rr[0].astype(F32)).astype(BF16)
    go("away", far_s, far_r, y_far)

    row, col = grid(64, 48)
    inner = row & 7
    spread = one_hot((over(row, 1, 3) * 6 + inner == col) & (inner < 6))
    total = ya[yl].astype(F32)
    for d in (1, 3, 2):
        got(f"ya{d}")
        total += yar[d - 1].astype(F32)
    za[...] = dot(spread, total.astype(BF16), 1, 0).astype(BF16).reshape(8, 8, WIDE)
    for d in (4, 3, 5, 2, 6, 1, 7):
        go(f"za{d}", za.at[lax.rem(z + d, 8)], zar.at[d - 1], z_of[d])
    total = zb[z].astype(F32)
    for d in (1, 7, 2, 6, 3, 5, 4):
        got(f"zb{d}")
        total += zbr[d - 1].astype(F32)
    yb[...] = dot(spread[0:32, 0:24], total.astype(BF16), 1, 0).astype(BF16).reshape(4, 8, LAST)
    for d in (2, 1, 3):
        go(f"yb{d}", yb.at[lax.rem(yl + d, 4)], ybr.at[d - 1], y_of[d])

    got("near", "away")
    sum_ref[...] = rf[3] + rr[1].astype(F32) + far_r[...].astype(F32)
    total = yb[yl].astype(F32)
    for d in (1, 3, 2):
        got(f"yb{d}")
        total += ybr[d - 1].astype(F32)
    gw_ref[2] = total[0:6, 0:GROUP]
    total = za[z].astype(F32)
    for d in (1, 7, 2, 6, 3, 5, 4):
        got(f"za{d}")
        total += zar[d - 1].astype(F32)
    for t in range(2):
        gw_ref[t] = total[0:6, GROUP * t : GROUP * (t + 1)]

    for name in NAMES:
        live[name].wait_send()


def shards(inputs, weight, grad_out):
    vmem = pl.BlockSpec(memory_space=pltpu.VMEM)
    count = len(NAMES)
    act, total, grad_weight = pl.pallas_call(
        kernel,
        out_shape=(
            jax.ShapeDtypeStruct((GROUP, COLS), F32),
            jax.ShapeDtypeStruct((GROUP, COLS), F32),
            jax.ShapeDtypeStruct((3, 6, GROUP), F32),
        ),
        in_specs=[vmem] * 3,
        out_specs=(vmem,) * 3,
        scratch_shapes=[
            pltpu.VMEM((3, 2, 2, GROUP, COLS), BF16),
            pltpu.VMEM((3, 4, 2, 2, 48, COLS), BF16),
            pltpu.VMEM((3, GROUP, 768), BF16),
            pltpu.VMEM((3, 4, GROUP, GROUP), BF16),
            pltpu.VMEM((3, GROUP, COLS), BF16),
            pltpu.VMEM((4, COLS, COLS), BF16),
            pltpu.VMEM((4, COLS, COLS), BF16),
            pltpu.VMEM((4, 48, WIDE), BF16),
            pltpu.VMEM((3, 48, WIDE), BF16),
            pltpu.VMEM((8, 8, WIDE), BF16),
            pltpu.VMEM((7, 8, WIDE), BF16),
            pltpu.VMEM((8, 24, LAST), BF16),
            pltpu.VMEM((7, 24, LAST), BF16),
            pltpu.VMEM((4, 8, LAST), BF16),
            pltpu.VMEM((3, 8, LAST), BF16),
            pltpu.VMEM((4, GROUP, COLS), F32),
            pltpu.VMEM((2, GROUP, COLS), BF16),
            pltpu.VMEM((2, GROUP, COLS), BF16),
            pltpu.VMEM((GROUP, COLS), BF16),
            pltpu.VMEM((GROUP, COLS), BF16),
            pltpu.SemaphoreType.DMA((count,)),
            pltpu.SemaphoreType.DMA((count,)),
        ],
        compiler_params=pltpu.CompilerParams(collective_id=0, has_side_effects=True),
    )(inputs, weight, grad_out)
    scale = (inputs.shape[1] * lax.axis_size("seq")) ** (-0.5)
    return (inputs + act, grad_out + total, grad_weight * scale)


def solution(mesh):
    return jax.shard_map(
        shards,
        mesh=mesh,
        in_specs=(P("ch", "seq"), P(None, "ch", None), P("ch", "seq")),
        out_specs=(P("ch", "seq"), P("ch", "seq"), P(None, "seq", "ch")),
        check_vma=False,
    )
```

time: 1520 us -> 55.6 us (0.04)
  the two profiles are of different devices: /device:TPU:32 before, /device:TPU:1 now
where the time goes in v2:
time: 55.6 us; the launch traced here: 55.4 us
  Pallas kernels  51.7 us (93%)
  other arithmetic  2.99 us (5%)
  between operations  0.68 us (1%)
    pallas_call x1, Pallas kernels, shards(): pl.pallas_call(kernel, out_shape=(jax.ShapeDtypeStruct((GROUP, COLS), F32...  51.7 us
    add x2, other arithmetic, shards(): return (inputs + act, grad_out + total, grad_weight * scale)  2.38 us

profile of v2, /device:TPU:1, one launch (start us, length us, event | category | flops | bytes accessed | tf_op | source)
XLA Modules:
  0.0 55.4 jit_solution(14387262846761130201)
XLA Ops:
  0.6 0.0 copy-start
  0.6 51.7 %shard_map.58 = (f32[192,256]{1,0:T(8,128)}, f32[192,256]{1,0:T(8,128)}, f32[3,6,192]{2,1,0:T(8,128)}) custom-call(f32[192,256]{1,0:T(8,128)} %x_ref.1, bf16[3,192,768]{2,1,0:T(8,128)(2,1)} %w_ref.1, f32[192,256]{1,0:T(8,128)} %g_ref.1), custom_call_target="tpu_custom_call" | custom-call | tf_op jit(solution)/shard_map/pallas_call | solution.py:272
  52.4 0.0 copy-done
  52.4 0.0 copy-start.3
  52.4 0.0 copy-start.1
  52.4 0.0 copy-start.2
  52.4 1.7 %add.6 = f32[192,256]{1,0:T(8,128)} add(f32[192,256]{1,0:T(8,128)S(1)} %copy-done, f32[192,256]{1,0:T(8,128)} %get-tuple-element.6) | non-fusion elementwise | flops 49152 | bytes 589824 | tf_op jit(solution)/shard_map/add | solution.py:308
  54.1 0.0 copy-done.3
  54.1 0.6 %broadcast_multiply_fusion = f32[3,6,192]{2,1,0:T(8,128)} fusion(f32[3,6,192]{2,1,0:T(8,128)S(1)} %copy-done.3), kind=kLoop, calls=%fused_computation | loop fusion | flops 3456 | bytes 27648 | tf_op jit(solution)/shard_map/mul | solution.py:308
  54.7 0.0 copy-done.1
  54.7 0.0 copy-done.2
  54.7 0.7 %add.7 = f32[192,256]{1,0:T(8,128)} add(f32[192,256]{1,0:T(8,128)S(1)} %copy-done.1, f32[192,256]{1,0:T(8,128)S(1)} %copy-done.2) | non-fusion elementwise | flops 49152 | bytes 589824 | tf_op jit(solution)/shard_map/add | solution.py:308
Async XLA Ops:
  0.6 51.7 %copy-start = (f32[192,256]{1,0:T(8,128)S(1)}, f32[192,256]{1,0:T(8,128)}, u32[]{:S(2)}) copy-start(f32[192,256]{1,0:T(8,128)} %x_ref.1) | copy-start | bytes 589828
  52.4 1.7 %copy-start.3 = (f32[3,6,192]{2,1,0:T(8,128)S(1)}, f32[3,6,192]{2,1,0:T(8,128)}, u32[]{:S(2)}) copy-start(f32[3,6,192]{2,1,0:T(8,128)} %get-tuple-element.8) | copy-start | bytes 41476
  52.4 2.3 %copy-start.1 = (f32[192,256]{1,0:T(8,128)S(1)}, f32[192,256]{1,0:T(8,128)}, u32[]{:S(2)}) copy-start(f32[192,256]{1,0:T(8,128)} %g_ref.1) | copy-start | bytes 589828
  52.4 2.3 %copy-start.2 = (f32[192,256]{1,0:T(8,128)S(1)}, f32[192,256]{1,0:T(8,128)}, u32[]{:S(2)}) copy-start(f32[192,256]{1,0:T(8,128)} %get-tuple-element.7) | copy-start | bytes 589828

commit v3 on v2

v3 whole, which is shorter than its diff:
```python
import math

import jax
import jax.numpy as jnp
from jax import lax
from jax.experimental import pallas as pl
from jax.experimental.pallas import tpu as pltpu
from jax.sharding import PartitionSpec as P

MESH = pl.DeviceIdType.MESH
F32, BF16 = jnp.float32, jnp.bfloat16
GROUP = 192
HALF = GROUP // 2
COLS = 256
WIDE = 384
LAST = 256
CHUNKS = 4
CHUNK = GROUP // CHUNKS

NAMES = ["own", "near", "co", "cf", "ci", "ct"]
for k in range(CHUNKS):
    NAMES += [f"{n}{k}" for n in ("up", "dn", "zu", "zd", "cup", "cdn", "czu", "czd", "r", "cr")]
for k in range(2):
    NAMES += [f"{n}{k}" for n in ("dy", "dz", "far", "away")]
for d in range(1, 4):
    NAMES += [f"{n}{d}" for n in ("so", "sf", "si", "st", "dx", "ya", "yb")]
for d in range(1, 8):
    NAMES += [f"za{d}", f"zb{d}"]
SLOT = {name: i for i, name in enumerate(NAMES)}


def dot(a, b, ca, cb):
    return lax.dot_general(a, b, (((ca,), (cb,)), ((), ())), preferred_element_type=F32)


def one_hot(hit):
    return jnp.where(hit, 1.0, 0.0).astype(BF16)


def grid(rows, cols):
    return [lax.broadcasted_iota(jnp.int32, (rows, cols), axis) for axis in range(2)]


def over(value, factor, bits):
    return lax.shift_right_logical(value * factor, bits)


def kernel(
    scale, x_hbm, w_hbm, g_hbm, out_ref, gin_ref, gw_ref,
    x_ref, w_ref, g_ref, xb, xs, wp, wt, db, dx, dlow, ya, yar, za, zar, zb, zbr, yb, ybr, rf, rb, rr, far_s, far_r, load, send, recv,
):
    loads = [pltpu.make_async_copy(a, b, load.at[i]) for i, (a, b) in enumerate(((x_hbm, x_ref), (w_hbm, w_ref), (g_hbm, g_ref)))]
    for one in loads:
        one.start()
    s, ch = lax.axis_index("seq"), lax.axis_index("ch")
    z, yl, x = lax.div(s, 16), lax.rem(lax.div(s, 4), 4), lax.rem(s, 4)
    yh, c = lax.div(ch, 2), lax.rem(ch, 2)
    y = yh * 4 + yl
    late = lax.div(yl, 2)

    def at(z, y, x, c):
        z, y, x = lax.rem(z, 8), lax.rem(y, 8), lax.rem(x, 4)
        return (z * 16 + lax.rem(y, 4) * 4 + x, lax.div(y, 4) * 2 + c)

    core = at(z, y, x, 1 - c)
    y_up, y_dn, y_far = at(z, y + 2, x, c), at(z, y + 6, x, c), at(z, y + 4, x, c)
    y_in = at(z, yh * 4 + lax.rem(yl + 2, 4), x, c)
    z_to = at(z + 1 + 6 * late, y, x, c)
    x_of = [None] + [at(z, y, x + d, c) for d in range(1, 4)]
    y_of = [None] + [at(z, yh * 4 + lax.rem(yl + d, 4), x, c) for d in range(1, 4)]
    z_of = [None] + [at(z + d, y, x, c) for d in range(1, 8)]

    barrier = pltpu.get_barrier_semaphore()
    peers = [core, y_up, y_dn, y_far] + x_of[1:] + y_of[1:] + z_of[1:]
    for peer in peers:
        pl.semaphore_signal(barrier, inc=1, device_id=peer, device_id_type=MESH)

    live = {}

    def go(name, src, dst, to):
        i = SLOT[name]
        live[name] = pltpu.make_async_remote_copy(
            src_ref=src, dst_ref=dst, send_sem=send.at[i], recv_sem=recv.at[i], device_id=to, device_id_type=MESH
        )
        live[name].start()

    def got(*names):
        for name in names:
            live[name].wait_recv()

    def ordering(size):
        row, col = grid(size, size)
        upper = jnp.where(row >= GROUP, 1, 0)
        r = row - GROUP * upper
        six = over(r, 10923, 16)
        source = (six & 1) * 96 + (over(six, 1, 1) & 3) * 24 + over(six, 1, 3) * 6 + r - six * 6
        return one_hot(source + GROUP * upper == col)

    order = ordering(GROUP)
    loads[0].wait()
    xb[1, yh, c] = dot(order, x_ref[...].astype(BF16), 1, 0).astype(BF16)

    pl.semaphore_wait(barrier, len(peers))

    t_to = 2 * late
    t_in = 2 - 2 * late
    piece = [pl.ds(CHUNK * k, CHUNK) for k in range(CHUNKS)]
    part = [pl.ds(HALF * k, HALF) for k in range(2)]
    h_dn, h_up, h_far = lax.div(lax.rem(y + 6, 8), 4), lax.div(lax.rem(y + 2, 8), 4), 1 - yh
    pairs = [(k, CHUNKS - 1 - k) for k in range(CHUNKS)]
    for k, m in pairs:
        go(f"up{k}", xb.at[1, yh, c, piece[k]], xb.at[t_to, yh, c, piece[k]], y_up)
        go(f"dn{m}", xb.at[1, yh, c, piece[m]], xb.at[t_to, yh, c, piece[m]], y_dn)
    go("own", xb.at[1, yh, c], xb.at[1, yh, c], core)

    def slices(d):
        return pl.ds(pl.multiple_of(lax.rem(x + d, 4) * 48, 48), 48)

    for d in (1, 3, 2):
        go(f"so{d}", xb.at[1, yh, c, slices(d)], xs.at[1, d, yh, c], x_of[d])

    order = ordering(WIDE)
    loads[1].wait()
    loads[2].wait()
    for t in range(3):
        for b in range(2):
            cols = slice(WIDE * b, WIDE * (b + 1))
            wp[t, :, cols] = dot(w_ref[t, :, cols], order, 1, 1).astype(BF16)

    for k, m in pairs:
        got(f"up{k}")
        block = xb.at[t_in, h_dn, c, piece[k]]
        go(f"zu{k}", block, xb.at[t_to, h_dn, c, piece[k]], z_to)
        if k < m:
            go(f"r{k}", block, xb.at[1, h_dn, c, piece[k]], y_up)
        got(f"dn{m}")
        other = xb.at[t_in, h_up, c, piece[m]]
        go(f"zd{m}", other, xb.at[t_to, h_up, c, piece[m]], z_to)
        if k < m:
            go(f"r{m}", other, xb.at[1, h_up, c, piece[m]], y_dn)
        go(f"cup{k}", block, block, core)
        go(f"cdn{m}", other, other, core)
    for d in (1, 3, 2):
        go(f"si{d}", xb.at[t_in, :, c, slices(d)], xs.at[t_in, d, :, c], x_of[d])
    wide = w_ref[...]
    for t in range(3):
        wt[t] = wide[t].T.reshape(4, GROUP, GROUP)
    got("so1", "so3", "so2")
    go("co", xs.at[1, 1:4, yh, c], xs.at[1, 1:4, yh, c], core)
    for k, m in pairs:
        got(f"zu{k}")
        block = xb.at[t_to, h_dn, c, piece[k]]
        go(f"czu{k}", block, block, core)
        got(f"zd{m}")
        block = xb.at[t_to, h_up, c, piece[m]]
        go(f"czd{m}", block, block, core)
        if k < m:
            for n in (k, m):
                got(f"r{n}")
                block = xb.at[1, h_far, c, piece[n]]
                go(f"cr{n}", block, block, core)
    for d in (1, 3, 2):
        go(f"st{d}", xb.at[t_to, :, c, slices(d)], xs.at[t_to, d, :, c], x_of[d])
        go(f"sf{d}", xb.at[1, h_far, c, slices(d)], xs.at[1, d, h_far, c], x_of[d])

    def tap(t):
        return dot(wp[t], xb[t].reshape(768, COLS), 1, 0)

    edge = jnp.where((s < 8) | (s >= 120), 0.0, 1.0).astype(F32)
    got("own", *[f"{name}{k}" for k in range(CHUNKS) for name in ("cup", "cdn", "cr")])
    preact = tap(1) + tap(t_in)
    got(*[f"{name}{k}" for k in range(CHUNKS) for name in ("czu", "czd")])
    preact += tap(t_to) * edge
    cdf = 0.5 * (1.0 + lax.erf(preact * (1.0 / math.sqrt(2.0))))
    pdf = jnp.exp(-0.5 * preact * preact) * (1.0 / math.sqrt(2.0 * math.pi))
    delta = (g_ref[...] * (cdf + preact * pdf)).astype(BF16)
    db[1] = delta
    dx[0, 0:GROUP] = delta

    for k in range(2):
        go(f"dy{k}", db.at[1, part[k]], db.at[t_to, part[k]], y_in)
    for d in (1, 3, 2):
        go(f"dx{d}", db.at[1], dx.at[d, 0:GROUP], x_of[d])
    out_ref[...] = x_ref[...] + preact * cdf
    got("si1", "si3", "si2")
    go("ci", xs.at[t_in, 1:4, :, c], xs.at[t_in, 1:4, :, c], core)
    got("sf1", "sf3", "sf2")
    go("cf", xs.at[1, 1:4, h_far, c], xs.at[1, 1:4, h_far, c], core)
    got("st1", "st3", "st2")
    go("ct", xs.at[t_to, 1:4, :, c], xs.at[t_to, 1:4, :, c], core)

    blocks = [(1 - yh) * 2 + 1 - c, (1 - yh) * 2 + c, yh * 2 + 1 - c, yh * 2 + c]
    for i, q in enumerate(blocks):
        rf[i] = dot(wt[1, q], delta, 1, 0)
    for d in range(4):
        dx[d, GROUP:COLS] = jnp.zeros((COLS - GROUP, COLS), BF16)
        dlow[d, 0:GROUP] = jnp.zeros((GROUP, COLS), BF16)
    for k in range(2):
        got(f"dy{k}")
        go(f"dz{k}", db.at[t_in, part[k]], db.at[t_to, part[k]], z_to)
    for i, q in enumerate(blocks):
        rf[i] += dot(wt[2 - t_in, q], db[t_in], 1, 0)

    first = jnp.where(s < 8, 0.0, 1.0).astype(F32)
    last = jnp.where(s >= 120, 0.0, 1.0).astype(F32)
    own_rows = slices(0)
    got("co", "ci", "cf", "ct")
    row, col = grid(GROUP, GROUP)
    twelve = over(row, 5462, 16)
    to_y = one_hot((twelve & 3) * 48 + over(twelve, 1, 2) * 12 + row - twelve * 12 == col)
    six = over(row, 10923, 16)
    at_z = over(six, 1, 2)
    to_z = one_hot(over(at_z, 1, 1) * 48 + (six & 3) * 12 + (at_z & 1) * 6 + row - six * 6 == col)

    def rows_of(t, d):
        return (xb[t, :, :, own_rows, :] if d == 0 else xs[t, d]).reshape(GROUP, COLS)

    sums = None
    for d in (0, 1, 3, 2):
        if d:
            got(f"dx{d}")
        dlow[d, GROUP:COLS] = dx[d, 0:64]
        here = rows_of(1, d)
        new = [dot(rows_of(0, d), dx[d], 1, 1), dot(here, dlow[d], 1, 1), dot(here, dx[d, 64:GROUP], 1, 1)]
        sums = new if sums is None else [a + b for a, b in zip(sums, new)]
    zb[:, :, 0:256] = dot(to_z, (sums[0] * first + sums[1]).astype(BF16), 1, 0).astype(BF16).reshape(8, 24, 256)
    zb[:, :, 256:WIDE] = dot(to_z, sums[2].astype(BF16), 1, 0).astype(BF16).reshape(8, 24, 128)
    for d in (4, 3, 5, 2, 6, 1, 7):
        go(f"zb{d}", zb.at[lax.rem(z + d, 8)], zbr.at[d - 1], z_of[d])
    third = dot(rows_of(2, 0), dx[0], 1, 1)
    for d in range(1, 4):
        third += dot(rows_of(2, d), dx[d], 1, 1)
    ya[...] = dot(to_y, (third * last).astype(BF16), 1, 0).astype(BF16).reshape(4, 48, LAST)
    for d in (2, 1, 3):
        go(f"ya{d}", ya.at[lax.rem(yl + d, 4)], yar.at[d - 1], y_of[d])

    got("dz0", "dz1")
    ends = [dot(wt[2 - t_to, q], db[t_to], 1, 0) * edge for q in blocks[:2]]
    for k in range(2):
        rows = slice(HALF * k, HALF * (k + 1))
        rb[0, rows] = (rf[0, rows] + ends[0][rows]).astype(BF16)
        go(f"far{k}", rb.at[0, part[k]], rr.at[0, part[k]], core)
    for k in range(2):
        rows = slice(HALF * k, HALF * (k + 1))
        mine = rf[1, rows] + ends[1][rows]
        got(f"far{k}")
        far_s[rows] = (mine + rr[0, rows].astype(F32)).astype(BF16)
        go(f"away{k}", far_s.at[part[k]], far_r.at[part[k]], y_far)
    rb[1] = (rf[2] + dot(wt[2 - t_to, blocks[2]], db[t_to], 1, 0) * edge).astype(BF16)
    go("near", rb.at[1], rr.at[1], core)
    rf[3] += dot(wt[2 - t_to, blocks[3]], db[t_to], 1, 0) * edge

    row, col = grid(64, 48)
    inner = row & 7
    spread = one_hot((over(row, 1, 3) * 6 + inner == col) & (inner < 6))
    total = ya[yl].astype(F32)
    for d in (1, 3, 2):
        got(f"ya{d}")
        total += yar[d - 1].astype(F32)
    za[...] = dot(spread, total.astype(BF16), 1, 0).astype(BF16).reshape(8, 8, LAST)
    for d in (4, 3, 5, 2, 6, 1, 7):
        go(f"za{d}", za.at[lax.rem(z + d, 8)], zar.at[d - 1], z_of[d])
    total = zb[z].astype(F32)
    for d in (1, 7, 2, 6, 3, 5, 4):
        got(f"zb{d}")
        total += zbr[d - 1].astype(F32)
    yb[...] = dot(spread[0:32, 0:24], total.astype(BF16), 1, 0).astype(BF16).reshape(4, 8, WIDE)
    for d in (2, 1, 3):
        go(f"yb{d}", yb.at[lax.rem(yl + d, 4)], ybr.at[d - 1], y_of[d])

    got("near", "away0", "away1")
    gin_ref[...] = g_ref[...] + (rf[3] + rr[1].astype(F32) + far_r[...].astype(F32))
    total = yb[yl].astype(F32)
    for d in (1, 3, 2):
        got(f"yb{d}")
        total += ybr[d - 1].astype(F32)
    total = total * scale
    for t in range(2):
        gw_ref[t] = total[0:6, GROUP * t : GROUP * (t + 1)]
    total = za[z].astype(F32)
    for d in (1, 7, 2, 6, 3, 5, 4):
        got(f"za{d}")
        total += zar[d - 1].astype(F32)
    gw_ref[2] = total[0:6, 0:GROUP] * scale

    for name in NAMES:
        live[name].wait_send()


def leave(*refs):
    held, left, done = refs[:3], refs[3:6], refs[6]
    copies = [pltpu.make_async_copy(a, b, done.at[i]) for i, (a, b) in enumerate(zip(held, left))]
    for one in copies:
        one.start()
    for one in copies:
        one.wait()


def shards(inputs, weight, grad_out):
    scale = (inputs.shape[1] * lax.axis_size("seq")) ** (-0.5)
    vmem, hbm = pl.BlockSpec(memory_space=pltpu.VMEM), pl.BlockSpec(memory_space=pltpu.HBM)
    count = len(NAMES)
    shapes = (
        jax.ShapeDtypeStruct((GROUP, COLS), F32),
        jax.ShapeDtypeStruct((GROUP, COLS), F32),
        jax.ShapeDtypeStruct((3, 6, GROUP), F32),
    )

    def body(*refs):
        kernel(scale, *refs)

    held = pl.pallas_call(
        body,
        out_shape=shapes,
        in_specs=[hbm] * 3,
        out_specs=(vmem,) * 3,
        scratch_shapes=[
            pltpu.VMEM((GROUP, COLS), F32),
            pltpu.VMEM((3, GROUP, 768), BF16),
            pltpu.VMEM((GROUP, COLS), F32),
            pltpu.VMEM((3, 2, 2, GROUP, COLS), BF16),
            pltpu.VMEM((3, 4, 2, 2, 48, COLS), BF16),
            pltpu.VMEM((3, GROUP, 768), BF16),
            pltpu.VMEM((3, 4, GROUP, GROUP), BF16),
            pltpu.VMEM((3, GROUP, COLS), BF16),
            pltpu.VMEM((4, COLS, COLS), BF16),
            pltpu.VMEM((4, COLS, COLS), BF16),
            pltpu.VMEM((4, 48, LAST), BF16),
            pltpu.VMEM((3, 48, LAST), BF16),
            pltpu.VMEM((8, 8, LAST), BF16),
            pltpu.VMEM((7, 8, LAST), BF16),
            pltpu.VMEM((8, 24, WIDE), BF16),
            pltpu.VMEM((7, 24, WIDE), BF16),
            pltpu.VMEM((4, 8, WIDE), BF16),
            pltpu.VMEM((3, 8, WIDE), BF16),
            pltpu.VMEM((4, GROUP, COLS), F32),
            pltpu.VMEM((2, GROUP, COLS), BF16),
            pltpu.VMEM((2, GROUP, COLS), BF16),
            pltpu.VMEM((GROUP, COLS), BF16),
            pltpu.VMEM((GROUP, COLS), BF16),
            pltpu.SemaphoreType.DMA((3,)),
            pltpu.SemaphoreType.DMA((count,)),
            pltpu.SemaphoreType.DMA((count,)),
        ],
        compiler_params=pltpu.CompilerParams(collective_id=0, has_side_effects=True, vmem_limit_bytes=20 * 2**20),
    )(*(pltpu.with_memory_space_constraint(a, pltpu.HBM) for a in (inputs, weight, grad_out)))
    return pl.pallas_call(
        leave,
        out_shape=shapes,
        in_specs=[vmem] * 3,
        out_specs=(hbm,) * 3,
        scratch_shapes=[pltpu.SemaphoreType.DMA((3,))],
        compiler_params=pltpu.CompilerParams(vmem_limit_bytes=4 * 2**20),
    )(*held)


def solution(mesh):
    return jax.shard_map(
        shards,
        mesh=mesh,
        in_specs=(P("ch", "seq"), P(None, "ch", None), P("ch", "seq")),
        out_specs=(P("ch", "seq"), P("ch", "seq"), P(None, "seq", "ch")),
        check_vma=False,
    )
```

time: 55.6 us -> 50.4 us (0.906)
  the two profiles are of different devices: /device:TPU:1 before, /device:TPU:8 now
where the time goes in v3:
time: 50.4 us; the launch traced here: 50.3 us
  Pallas kernels  49.6 us (98%)
  between operations  0.64 us (1%)
    pallas_call x1, Pallas kernels, shards(): pl.pallas_call(body, out_shape=shapes, in_specs=[hbm] * 3, out_specs=(vme...  48.9 us

profile of v3, /device:TPU:8, one launch (start us, length us, event | category | flops | bytes accessed | tf_op | source)
XLA Modules:
  0.0 50.3 jit_solution(18058979166687016935)
XLA Ops:
  0.6 48.9 %shard_map.58 = (f32[192,256]{1,0:T(8,128)S(1)}, f32[192,256]{1,0:T(8,128)S(1)}, f32[3,6,192]{2,1,0:T(8,128)S(1)}) custom-call(f32[192,256]{1,0:T(8,128)} %refs_0_.1, bf16[3,192,768]{2,1,0:T(8,128)(2,1)} %refs_1_.1, f32[192,256]{1,0:T(8,128)} %refs_2_.1), custom_call_target="tpu_custom_call" | custom-call | tf_op jit(solution)/shard_map/pallas_call | solution.py:312
  49.5 0.8 %shard_map.59 = (f32[192,256]{1,0:T(8,128)}, f32[192,256]{1,0:T(8,128)}, f32[3,6,192]{2,1,0:T(8,128)}) custom-call(f32[192,256]{1,0:T(8,128)S(1)} %get-tuple-element.6.refs_0_, f32[192,256]{1,0:T(8,128)S(1)} %get-tuple-element.7.refs_1_, f32[3,6,192]{2,1,0:T(8,128)S(1)} %get-tuple-element.8.refs_2_), custom_call_target="tpu_custom_call" | custom-call | tf_op jit(solution)/shard_map/pallas_call | solution.py:347

commit v4 on v3

v4 whole, which is shorter than its diff:
```python
import math

import jax
import jax.numpy as jnp
from jax import lax
from jax.experimental import pallas as pl
from jax.experimental.pallas import tpu as pltpu
from jax.sharding import PartitionSpec as P

MESH = pl.DeviceIdType.MESH
F32, BF16 = jnp.float32, jnp.bfloat16
GROUP = 192
HALF = GROUP // 2
COLS = 256
TILE = 128
WIDE = 384
LAST = 256
CHUNKS = 4
CHUNK = GROUP // CHUNKS

ARRIVALS = [f"{n}{k}" for n in ("up", "dn", "zu", "zd", "r") for k in range(CHUNKS)]
ARRIVALS += [f"{n}{k}" for n in ("dy0", "dy1", "dz", "far") for k in range(2)]
ARRIVALS += ["near", "away", "here", "next", "so", "si", "sf", "st", "co", "ci", "dx", "ya", "yb", "za", "zb"]
DEPARTURES = ["slabs", "rest", "slices", "grads", "sums", "dx", "ya", "yb", "za", "zb"]
ARRIVE = {name: i for i, name in enumerate(ARRIVALS)}
DEPART = {name: i for i, name in enumerate(DEPARTURES)}


def dot(a, b, ca, cb):
    return lax.dot_general(a, b, (((ca,), (cb,)), ((), ())), preferred_element_type=F32)


def one_hot(hit):
    return jnp.where(hit, 1.0, 0.0).astype(BF16)


def grid(rows, cols):
    return [lax.broadcasted_iota(jnp.int32, (rows, cols), axis) for axis in range(2)]


def over(value, factor, bits):
    return lax.shift_right_logical(value * factor, bits)


def kernel(
    scale, x_hbm, w_hbm, g_hbm, out_ref, gin_ref, gw_ref,
    x_ref, w_ref, g_ref, xb, xs, wp, wt, db, dx, dlow, ya, yar, za, zar, zb, zbr, yb, ybr, rf, rb, rr, far_s, far_r, load, send, recv,
):
    loads = [pltpu.make_async_copy(a, b, load.at[i]) for i, (a, b) in enumerate(((x_hbm, x_ref), (w_hbm, w_ref), (g_hbm, g_ref)))]
    loads[0].start()
    s, ch = lax.axis_index("seq"), lax.axis_index("ch")
    z, yl, x = lax.div(s, 16), lax.rem(lax.div(s, 4), 4), lax.rem(s, 4)
    yh, c = lax.div(ch, 2), lax.rem(ch, 2)
    y = yh * 4 + yl
    late = lax.div(yl, 2)

    def at(z, y, x, c):
        z, y, x = lax.rem(z, 8), lax.rem(y, 8), lax.rem(x, 4)
        return (z * 16 + lax.rem(y, 4) * 4 + x, lax.div(y, 4) * 2 + c)

    core = at(z, y, x, 1 - c)
    y_up, y_dn, y_far = at(z, y + 2, x, c), at(z, y + 6, x, c), at(z, y + 4, x, c)
    y_in = at(z, yh * 4 + lax.rem(yl + 2, 4), x, c)
    z_to = at(z + 1 + 6 * late, y, x, c)
    x_of = [None] + [at(z, y, x + d, c) for d in range(1, 4)]
    y_of = [None] + [at(z, yh * 4 + lax.rem(yl + d, 4), x, c) for d in range(1, 4)]
    z_of = [None] + [at(z + d, y, x, c) for d in range(1, 8)]

    barrier = pltpu.get_barrier_semaphore()
    peers = [core, y_up, y_dn, y_far] + x_of[1:] + y_of[1:] + z_of[1:]
    for peer in peers:
        pl.semaphore_signal(barrier, inc=1, device_id=peer, device_id_type=MESH)

    def copy(arrival, departure, src, dst, to):
        return pltpu.make_async_remote_copy(
            src_ref=src,
            dst_ref=dst,
            send_sem=send.at[DEPART[departure]],
            recv_sem=recv.at[ARRIVE[arrival]],
            device_id=to,
            device_id_type=MESH,
        )

    def go(arrival, departure, src, dst, to):
        copy(arrival, departure, src, dst, to).start()

    def got(arrival, whole):
        copy(arrival, "rest", whole, whole, core).wait_recv()

    def left(departure, whole):
        copy("near", departure, whole, whole, core).wait_send()

    def ordering(size):
        row, col = grid(size, size)
        upper = jnp.where(row >= GROUP, 1, 0)
        r = row - GROUP * upper
        six = over(r, 10923, 16)
        source = (over(six, 1, 2) & 1) * 96 + (six & 3) * 24 + over(six, 1, 3) * 6 + r - six * 6
        return one_hot(source + GROUP * upper == col)

    order = ordering(GROUP)
    loads[0].wait()
    loads[1].start()
    loads[2].start()
    xb[1, yh, c] = dot(order, x_ref[...].astype(BF16), 1, 0).astype(BF16)

    pl.semaphore_wait(barrier, len(peers))

    t_to = 2 * late
    t_in = 2 - 2 * late
    piece = [pl.ds(CHUNK * k, CHUNK) for k in range(CHUNKS)]
    part = [pl.ds(HALF * k, HALF) for k in range(2)]
    h_dn, h_up, h_far = lax.div(lax.rem(y + 6, 8), 4), lax.div(lax.rem(y + 2, 8), 4), 1 - yh
    pairs = [(k, CHUNKS - 1 - k) for k in range(CHUNKS)]
    for k, m in pairs:
        go(f"up{k}", "slabs", xb.at[1, yh, c, piece[k]], xb.at[t_to, yh, c, piece[k]], y_up)
        go(f"dn{m}", "slabs", xb.at[1, yh, c, piece[m]], xb.at[t_to, yh, c, piece[m]], y_dn)
    go("here", "rest", xb.at[1, yh, c], xb.at[1, yh, c], core)

    def slices(d):
        return pl.ds(pl.multiple_of(lax.rem(x + d, 4) * 48, 48), 48)

    for d in (1, 3, 2):
        go("so", "slices", xb.at[1, yh, c, slices(d)], xs.at[1, d, yh, c], x_of[d])

    order = ordering(WIDE)
    loads[1].wait()
    loads[2].wait()
    for t in range(3):
        for b in range(2):
            cols = slice(WIDE * b, WIDE * (b + 1))
            wp[t, :, cols] = dot(w_ref[t, :, cols], order, 1, 1).astype(BF16)

    slab_piece = xb.at[0, 0, 0, piece[0]]
    for k, m in pairs:
        got(f"up{k}", slab_piece)
        block = xb.at[t_in, h_dn, c, piece[k]]
        if k < m:
            go(f"r{k}", "rest", block, xb.at[1, h_dn, c, piece[k]], y_up)
        got(f"dn{m}", slab_piece)
        other = xb.at[t_in, h_up, c, piece[m]]
        if k < m:
            go(f"r{m}", "rest", other, xb.at[1, h_up, c, piece[m]], y_dn)
        go(f"zu{k}", "slabs", block, xb.at[t_to, h_dn, c, piece[k]], z_to)
        go(f"zd{m}", "slabs", other, xb.at[t_to, h_up, c, piece[m]], z_to)
        go("here", "slabs", block, block, core)
        go("here", "slabs", other, other, core)
    for d in (1, 3, 2):
        go("si", "slices", xb.at[t_in, :, c, slices(d)], xs.at[t_in, d, :, c], x_of[d])
    wide = w_ref[...]
    for t in range(3):
        wt[t] = wide[t].T.reshape(4, GROUP, GROUP)
    block = xs.at[1, 1:4, yh, c]
    got("so", block)
    go("co", "slices", block, block, core)
    for k, m in pairs:
        if k < m:
            for n in (k, m):
                got(f"r{n}", slab_piece)
                block = xb.at[1, h_far, c, piece[n]]
                go("here", "rest", block, block, core)
        got(f"zu{k}", slab_piece)
        block = xb.at[t_to, h_dn, c, piece[k]]
        go("next", "slabs", block, block, core)
        got(f"zd{m}", slab_piece)
        block = xb.at[t_to, h_up, c, piece[m]]
        go("next", "slabs", block, block, core)
    for d in (1, 3, 2):
        go("st", "slices", xb.at[t_to, :, c, slices(d)], xs.at[t_to, d, :, c], x_of[d])
        go("sf", "slices", xb.at[1, h_far, c, slices(d)], xs.at[1, d, h_far, c], x_of[d])

    def tap(t):
        return dot(wp[t], xb[t].reshape(768, COLS), 1, 0)

    edge = jnp.where((s < 8) | (s >= 120), 0.0, 1.0).astype(F32)
    got("here", xb.at[0])
    preact = tap(1) + tap(t_in)
    got("next", xb.at[0, 0])
    preact += tap(t_to) * edge
    cdf = 0.5 * (1.0 + lax.erf(preact * (1.0 / math.sqrt(2.0))))
    pdf = jnp.exp(-0.5 * preact * preact) * (1.0 / math.sqrt(2.0 * math.pi))
    delta = (g_ref[...] * (cdf + preact * pdf)).astype(BF16)
    for h in range(2):
        db[1, h] = delta[:, TILE * h : TILE * (h + 1)]
    dx[0, 0:GROUP] = delta

    for h in range(2):
        for k in range(2):
            go(f"dy{h}{k}", "grads", db.at[1, h, part[k]], db.at[t_to, h, part[k]], y_in)
    for d in (1, 3, 2):
        go("dx", "dx", dx.at[0, 0:GROUP], dx.at[d, 0:GROUP], x_of[d])
    out_ref[...] = x_ref[...] + preact * cdf
    for arrival, onward, block in (
        ("si", "ci", xs.at[t_in, 1:4, :, c]),
        ("sf", "co", xs.at[1, 1:4, h_far, c]),
        ("st", "ci", xs.at[t_to, 1:4, :, c]),
    ):
        got(arrival, block)
        go(onward, "slices", block, block, core)

    blocks = [(1 - yh) * 2 + 1 - c, (1 - yh) * 2 + c, yh * 2 + 1 - c, yh * 2 + c]
    for i, q in enumerate(blocks):
        back = dot(wt[1, q], delta, 1, 0)
        for h in range(2):
            rf[i, h] = back[:, TILE * h : TILE * (h + 1)]
    for d in range(4):
        dx[d, GROUP:COLS] = jnp.zeros((COLS - GROUP, COLS), BF16)
        dlow[d, 0:GROUP] = jnp.zeros((GROUP, COLS), BF16)
    for h in range(2):
        for k in range(2):
            got(f"dy{h}{k}", db.at[0, 0, part[0]])
            go(f"dz{h}", "grads", db.at[t_in, h, part[k]], db.at[t_to, h, part[k]], z_to)
        for i, q in enumerate(blocks):
            rf[i, h] += dot(wt[2 - t_in, q], db[t_in, h], 1, 0)

    first = jnp.where(s < 8, 0.0, 1.0).astype(F32)
    last = jnp.where(s >= 120, 0.0, 1.0).astype(F32)
    own_rows = slices(0)
    got("co", xs.at[1, 1:4, :, 0])
    got("ci", xs.at[0, 1:4])
    got("dx", dx.at[1:4, 0:GROUP])
    row, col = grid(GROUP, GROUP)
    six = over(row, 10923, 16)
    to_y = one_hot((six & 7) * 24 + over(six, 1, 3) * 6 + row - six * 6 == col)

    def rows_of(t, d):
        return (xb[t, :, :, own_rows, :] if d == 0 else xs[t, d]).reshape(GROUP, COLS)

    sums = None
    for d in (0, 1, 3, 2):
        dlow[d, GROUP:COLS] = dx[d, 0:64]
        here = rows_of(1, d)
        new = [dot(rows_of(0, d), dx[d], 1, 1), dot(here, dlow[d], 1, 1), dot(here, dx[d, 64:GROUP], 1, 1)]
        sums = new if sums is None else [a + b for a, b in zip(sums, new)]
    zb[:, :, 0:256] = (sums[0] * first + sums[1]).astype(BF16).reshape(8, 24, 256)
    zb[:, :, 256:WIDE] = sums[2].astype(BF16).reshape(8, 24, 128)
    for d in (4, 3, 5, 2, 6, 1, 7):
        go("zb", "zb", zb.at[lax.rem(z + d, 8)], zbr.at[d - 1], z_of[d])
    third = dot(rows_of(2, 0), dx[0], 1, 1)
    for d in range(1, 4):
        third += dot(rows_of(2, d), dx[d], 1, 1)
    ya[...] = dot(to_y, (third * last).astype(BF16), 1, 0).astype(BF16).reshape(4, 48, LAST)
    for d in (2, 1, 3):
        go("ya", "ya", ya.at[lax.rem(yl + d, 4)], yar.at[d - 1], y_of[d])

    for h in range(2):
        got(f"dz{h}", db.at[0, h])

        def whole(i):
            return rf[i, h] + dot(wt[2 - t_to, blocks[i]], db[t_to, h], 1, 0) * edge

        rb[0, h] = whole(0).astype(BF16)
        go(f"far{h}", "grads", rb.at[0, h], rr.at[0, h], core)
        mine = whole(1)
        rb[1, h] = whole(2).astype(BF16)
        go("near", "sums", rb.at[1, h], rr.at[1, h], core)
        rf[3, h] = whole(3)
        got(f"far{h}", rr.at[0, h])
        far_s[h] = (mine + rr[0, h].astype(F32)).astype(BF16)
        go("away", "sums", far_s.at[h], far_r.at[h], y_far)

    row, col = grid(64, 48)
    inner = row & 7
    spread = one_hot((over(row, 1, 3) * 6 + inner == col) & (inner < 6))
    total = ya[yl].astype(F32)
    got("ya", yar)
    for d in (1, 3, 2):
        total += yar[d - 1].astype(F32)
    za[...] = dot(spread, total.astype(BF16), 1, 0).astype(BF16).reshape(8, 8, LAST)
    for d in (4, 3, 5, 2, 6, 1, 7):
        go("za", "za", za.at[lax.rem(z + d, 8)], zar.at[d - 1], z_of[d])
    total = zb[z].astype(F32)
    got("zb", zbr)
    for d in (1, 7, 2, 6, 3, 5, 4):
        total += zbr[d - 1].astype(F32)
    yb[...] = dot(spread[0:32, 0:24], total.astype(BF16), 1, 0).astype(BF16).reshape(4, 8, WIDE)
    for d in (2, 1, 3):
        go("yb", "yb", yb.at[lax.rem(yl + d, 4)], ybr.at[d - 1], y_of[d])

    got("near", rr.at[1])
    left("slabs", xb.at[0:2])
    left("rest", xb.at[:, 0, 0])
    left("slices", xs.at[:, 0:3])
    left("dx", dx.at[1:4, 0:GROUP])
    left("grads", db)
    got("away", far_r)
    for h in range(2):
        cols = slice(TILE * h, TILE * (h + 1))
        gin_ref[:, cols] = g_ref[:, cols] + (rf[3, h] + rr[1, h].astype(F32) + far_r[h].astype(F32))
    total = yb[yl].astype(F32)
    got("yb", ybr)
    for d in (1, 3, 2):
        total += ybr[d - 1].astype(F32)
    total = total * scale
    for t in range(2):
        gw_ref[t] = total[0:6, GROUP * t : GROUP * (t + 1)]
    total = za[z].astype(F32)
    got("za", zar)
    for d in (1, 7, 2, 6, 3, 5, 4):
        total += zar[d - 1].astype(F32)
    gw_ref[2] = total[0:6, 0:GROUP] * scale

    left("sums", rr)
    left("ya", yar)
    left("yb", ybr)
    left("za", zar)
    left("zb", zbr)


def leave(*refs):
    held, left, done = refs[:3], refs[3:6], refs[6]
    copies = [pltpu.make_async_copy(a, b, done.at[i]) for i, (a, b) in enumerate(zip(held, left))]
    for one in copies:
        one.start()
    for one in copies:
        one.wait()


def shards(inputs, weight, grad_out):
    scale = (inputs.shape[1] * lax.axis_size("seq")) ** (-0.5)
    vmem, hbm = pl.BlockSpec(memory_space=pltpu.VMEM), pl.BlockSpec(memory_space=pltpu.HBM)
    shapes = (
        jax.ShapeDtypeStruct((GROUP, COLS), F32),
        jax.ShapeDtypeStruct((GROUP, COLS), F32),
        jax.ShapeDtypeStruct((3, 6, GROUP), F32),
    )

    def body(*refs):
        kernel(scale, *refs)

    held = pl.pallas_call(
        body,
        out_shape=shapes,
        in_specs=[hbm] * 3,
        out_specs=(vmem,) * 3,
        scratch_shapes=[
            pltpu.VMEM((GROUP, COLS), F32),
            pltpu.VMEM((3, GROUP, 768), BF16),
            pltpu.VMEM((GROUP, COLS), F32),
            pltpu.VMEM((3, 2, 2, GROUP, COLS), BF16),
            pltpu.VMEM((3, 4, 2, 2, 48, COLS), BF16),
            pltpu.VMEM((3, GROUP, 768), BF16),
            pltpu.VMEM((3, 4, GROUP, GROUP), BF16),
            pltpu.VMEM((3, 2, GROUP, TILE), BF16),
            pltpu.VMEM((4, COLS, COLS), BF16),
            pltpu.VMEM((4, COLS, COLS), BF16),
            pltpu.VMEM((4, 48, LAST), BF16),
            pltpu.VMEM((3, 48, LAST), BF16),
            pltpu.VMEM((8, 8, LAST), BF16),
            pltpu.VMEM((7, 8, LAST), BF16),
            pltpu.VMEM((8, 24, WIDE), BF16),
            pltpu.VMEM((7, 24, WIDE), BF16),
            pltpu.VMEM((4, 8, WIDE), BF16),
            pltpu.VMEM((3, 8, WIDE), BF16),
            pltpu.VMEM((4, 2, GROUP, TILE), F32),
            pltpu.VMEM((2, 2, GROUP, TILE), BF16),
            pltpu.VMEM((2, 2, GROUP, TILE), BF16),
            pltpu.VMEM((2, GROUP, TILE), BF16),
            pltpu.VMEM((2, GROUP, TILE), BF16),
            pltpu.SemaphoreType.DMA((3,)),
            pltpu.SemaphoreType.DMA((len(DEPARTURES),)),
            pltpu.SemaphoreType.DMA((len(ARRIVALS),)),
        ],
        compiler_params=pltpu.CompilerParams(collective_id=0, has_side_effects=True, vmem_limit_bytes=20 * 2**20),
    )(*(pltpu.with_memory_space_constraint(a, pltpu.HBM) for a in (inputs, weight, grad_out)))
    return pl.pallas_call(
        leave,
        out_shape=shapes,
        in_specs=[vmem] * 3,
        out_specs=(hbm,) * 3,
        scratch_shapes=[pltpu.SemaphoreType.DMA((3,))],
        compiler_params=pltpu.CompilerParams(vmem_limit_bytes=4 * 2**20),
    )(*held)


def solution(mesh):
    return jax.shard_map(
        shards,
        mesh=mesh,
        in_specs=(P("ch", "seq"), P(None, "ch", None), P("ch", "seq")),
        out_specs=(P("ch", "seq"), P("ch", "seq"), P(None, "seq", "ch")),
        check_vma=False,
    )
```

time: 50.4 us -> 48.7 us (0.966)
  Pallas kernels: 49.6 us -> 48 us
    pallas_call x1, Pallas kernels: 48.9 us -> 47.2 us  [shards(): pl.pallas_call(body, out_shape=shapes, in_specs=[hbm] * 3, out_specs=(vme...]
where the time goes in v4:
time: 48.7 us; the launch traced here: 48.6 us
  Pallas kernels  48 us (99%)
  between operations  0.64 us (1%)
    pallas_call x1, Pallas kernels, shards(): pl.pallas_call(body, out_shape=shapes, in_specs=[hbm] * 3, out_specs=(vme...  47.2 us

profile of v4, /device:TPU:8, one launch (start us, length us, event | category | flops | bytes accessed | tf_op | source)
XLA Modules:
  0.0 48.6 jit_solution(2824525304972950933)
XLA Ops:
  0.6 47.2 %shard_map.58 = (f32[192,256]{1,0:T(8,128)S(1)}, f32[192,256]{1,0:T(8,128)S(1)}, f32[3,6,192]{2,1,0:T(8,128)S(1)}) custom-call(f32[192,256]{1,0:T(8,128)} %refs_0_.1, bf16[3,192,768]{2,1,0:T(8,128)(2,1)} %refs_1_.1, f32[192,256]{1,0:T(8,128)} %refs_2_.1), custom_call_target="tpu_custom_call" | custom-call | tf_op jit(solution)/shard_map/pallas_call | solution.py:331
  47.8 0.8 %shard_map.59 = (f32[192,256]{1,0:T(8,128)}, f32[192,256]{1,0:T(8,128)}, f32[3,6,192]{2,1,0:T(8,128)}) custom-call(f32[192,256]{1,0:T(8,128)S(1)} %get-tuple-element.6.refs_0_, f32[192,256]{1,0:T(8,128)S(1)} %get-tuple-element.7.refs_1_, f32[3,6,192]{2,1,0:T(8,128)S(1)} %get-tuple-element.8.refs_2_), custom_call_target="tpu_custom_call" | custom-call | tf_op jit(solution)/shard_map/pallas_call | solution.py:366

commit v5 on v4

--- a/solution.py
+++ b/solution.py
@@ -20,7 +20,7 @@
 
 ARRIVALS = [f"{n}{k}" for n in ("up", "dn", "zu", "zd", "r") for k in range(CHUNKS)]
 ARRIVALS += [f"{n}{k}" for n in ("dy0", "dy1", "dz", "far") for k in range(2)]
-ARRIVALS += ["near", "away", "here", "next", "so", "si", "sf", "st", "co", "ci", "dx", "ya", "yb", "za", "zb"]
+ARRIVALS += ["near", "away", "here", "over", "next", "so", "si", "sf", "st", "co", "ci", "dx1", "dx2", "dx3", "ya", "yb", "za", "zb"]
 DEPARTURES = ["slabs", "rest", "slices", "grads", "sums", "dx", "ya", "yb", "za", "zb"]
 ARRIVE = {name: i for i, name in enumerate(ARRIVALS)}
 DEPART = {name: i for i, name in enumerate(DEPARTURES)}
@@ -158,25 +158,34 @@
             for n in (k, m):
                 got(f"r{n}", slab_piece)
                 block = xb.at[1, h_far, c, piece[n]]
-                go("here", "rest", block, block, core)
+                go("over", "rest", block, block, core)
+            if k + 1 == m:
+                for d in (1, 3, 2):
+                    go("sf", "slices", xb.at[1, h_far, c, slices(d)], xs.at[1, d, h_far, c], x_of[d])
         got(f"zu{k}", slab_piece)
         block = xb.at[t_to, h_dn, c, piece[k]]
         go("next", "slabs", block, block, core)
         got(f"zd{m}", slab_piece)
         block = xb.at[t_to, h_up, c, piece[m]]
         go("next", "slabs", block, block, core)
-    for d in (1, 3, 2):
-        go("st", "slices", xb.at[t_to, :, c, slices(d)], xs.at[t_to, d, :, c], x_of[d])
-        go("sf", "slices", xb.at[1, h_far, c, slices(d)], xs.at[1, d, h_far, c], x_of[d])
-
     def tap(t):
         return dot(wp[t], xb[t].reshape(768, COLS), 1, 0)
 
     edge = jnp.where((s < 8) | (s >= 120), 0.0, 1.0).astype(F32)
-    got("here", xb.at[0])
-    preact = tap(1) + tap(t_in)
+    def half(h):
+        cols = pl.ds(pl.multiple_of(h * WIDE, TILE), WIDE)
+        return dot(wp[1, :, cols], xb[1, h].reshape(WIDE, COLS), 1, 0)
+
+    got("here", xb.at[:, 0, 0])
+    preact = half(yh) + tap(t_in)
     got("next", xb.at[0, 0])
     preact += tap(t_to) * edge
+    block = xs.at[t_in, 1:4, :, c]
+    got("si", block)
+    go("st", "slices", block, xs.at[t_to, 1:4, :, c], z_to)
+    go("ci", "slices", block, block, core)
+    got("over", xb.at[0, 0, 0])
+    preact += half(h_far)
     cdf = 0.5 * (1.0 + lax.erf(preact * (1.0 / math.sqrt(2.0))))
     pdf = jnp.exp(-0.5 * preact * preact) * (1.0 / math.sqrt(2.0 * math.pi))
     delta = (g_ref[...] * (cdf + preact * pdf)).astype(BF16)
@@ -188,16 +197,8 @@
         for k in range(2):
             go(f"dy{h}{k}", "grads", db.at[1, h, part[k]], db.at[t_to, h, part[k]], y_in)
     for d in (1, 3, 2):
-        go("dx", "dx", dx.at[0, 0:GROUP], dx.at[d, 0:GROUP], x_of[d])
+        go(f"dx{d}", "dx", dx.at[0, 0:GROUP], dx.at[d, 0:GROUP], x_of[d])
     out_ref[...] = x_ref[...] + preact * cdf
-    for arrival, onward, block in (
-        ("si", "ci", xs.at[t_in, 1:4, :, c]),
-        ("sf", "co", xs.at[1, 1:4, h_far, c]),
-        ("st", "ci", xs.at[t_to, 1:4, :, c]),
-    ):
-        got(arrival, block)
-        go(onward, "slices", block, block, core)
-
     blocks = [(1 - yh) * 2 + 1 - c, (1 - yh) * 2 + c, yh * 2 + 1 - c, yh * 2 + c]
     for i, q in enumerate(blocks):
         back = dot(wt[1, q], delta, 1, 0)
@@ -206,6 +207,24 @@
     for d in range(4):
         dx[d, GROUP:COLS] = jnp.zeros((COLS - GROUP, COLS), BF16)
         dlow[d, 0:GROUP] = jnp.zeros((GROUP, COLS), BF16)
+    own_rows = slices(0)
+
+    def rows_of(t, d):
+        return (xb[t, :, :, own_rows, :] if d == 0 else xs[t, d]).reshape(GROUP, COLS)
+
+    def products(d):
+        dlow[d, GROUP:COLS] = dx[d, 0:64]
+        here = rows_of(1, d)
+        wide, low, high = dx[d], dlow[d], dx[d, 64:GROUP]
+        return [dot(rows_of(0, d), wide, 1, 1), dot(here, low, 1, 1), dot(here, high, 1, 1), dot(rows_of(2, d), wide, 1, 1)]
+
+    sums = products(0)
+    for arrival, onward, block in (
+        ("sf", "co", xs.at[1, 1:4, h_far, c]),
+        ("st", "ci", xs.at[t_to, 1:4, :, c]),
+    ):
+        got(arrival, block)
+        go(onward, "slices", block, block, core)
     for h in range(2):
         for k in range(2):
             got(f"dy{h}{k}", db.at[0, 0, part[0]])
@@ -215,31 +234,20 @@
 
     first = jnp.where(s < 8, 0.0, 1.0).astype(F32)
     last = jnp.where(s >= 120, 0.0, 1.0).astype(F32)
-    own_rows = slices(0)
     got("co", xs.at[1, 1:4, :, 0])
     got("ci", xs.at[0, 1:4])
-    got("dx", dx.at[1:4, 0:GROUP])
     row, col = grid(GROUP, GROUP)
     six = over(row, 10923, 16)
     to_y = one_hot((six & 7) * 24 + over(six, 1, 3) * 6 + row - six * 6 == col)
 
-    def rows_of(t, d):
-        return (xb[t, :, :, own_rows, :] if d == 0 else xs[t, d]).reshape(GROUP, COLS)
-
-    sums = None
-    for d in (0, 1, 3, 2):
-        dlow[d, GROUP:COLS] = dx[d, 0:64]
-        here = rows_of(1, d)
-        new = [dot(rows_of(0, d), dx[d], 1, 1), dot(here, dlow[d], 1, 1), dot(here, dx[d, 64:GROUP], 1, 1)]
-        sums = new if sums is None else [a + b for a, b in zip(sums, new)]
+    for d in (1, 3, 2):
+        got(f"dx{d}", dx.at[1, 0:GROUP])
+        sums = [a + b for a, b in zip(sums, products(d))]
     zb[:, :, 0:256] = (sums[0] * first + sums[1]).astype(BF16).reshape(8, 24, 256)
     zb[:, :, 256:WIDE] = sums[2].astype(BF16).reshape(8, 24, 128)
     for d in (4, 3, 5, 2, 6, 1, 7):
         go("zb", "zb", zb.at[lax.rem(z + d, 8)], zbr.at[d - 1], z_of[d])
-    third = dot(rows_of(2, 0), dx[0], 1, 1)
-    for d in range(1, 4):
-        third += dot(rows_of(2, d), dx[d], 1, 1)
-    ya[...] = dot(to_y, (third * last).astype(BF16), 1, 0).astype(BF16).reshape(4, 48, LAST)
+    ya[...] = dot(to_y, (sums[3] * last).astype(BF16), 1, 0).astype(BF16).reshape(4, 48, LAST)
     for d in (2, 1, 3):
         go("ya", "ya", ya.at[lax.rem(yl + d, 4)], yar.at[d - 1], y_of[d])
 

time: 48.7 us -> 46.3 us (0.951)
  Pallas kernels: 48 us -> 45.6 us
    pallas_call x1, Pallas kernels: 47.2 us -> 44.8 us  [shards(): pl.pallas_call(body, out_shape=shapes, in_specs=[hbm] * 3, out_specs=(vme...]
where the time goes in v5:
time: 46.3 us; the launch traced here: 46.2 us
  Pallas kernels  45.6 us (98%)
  between operations  0.64 us (1%)
    pallas_call x1, Pallas kernels, shards(): pl.pallas_call(body, out_shape=shapes, in_specs=[hbm] * 3, out_specs=(vme...  44.8 us

profile of v5, /device:TPU:8, one launch (start us, length us, event | category | flops | bytes accessed | tf_op | source)
XLA Modules:
  0.0 46.2 jit_solution(2063508659840246100)
XLA Ops:
  0.6 44.8 %shard_map.58 = (f32[192,256]{1,0:T(8,128)S(1)}, f32[192,256]{1,0:T(8,128)S(1)}, f32[3,6,192]{2,1,0:T(8,128)S(1)}) custom-call(f32[192,256]{1,0:T(8,128)} %refs_0_.1, bf16[3,192,768]{2,1,0:T(8,128)(2,1)} %refs_1_.1, f32[192,256]{1,0:T(8,128)} %refs_2_.1), custom_call_target="tpu_custom_call" | custom-call | tf_op jit(solution)/shard_map/pallas_call | solution.py:339
  45.4 0.8 %shard_map.59 = (f32[192,256]{1,0:T(8,128)}, f32[192,256]{1,0:T(8,128)}, f32[3,6,192]{2,1,0:T(8,128)}) custom-call(f32[192,256]{1,0:T(8,128)S(1)} %get-tuple-element.6.refs_0_, f32[192,256]{1,0:T(8,128)S(1)} %get-tuple-element.7.refs_1_, f32[3,6,192]{2,1,0:T(8,128)S(1)} %get-tuple-element.8.refs_2_), custom_call_target="tpu_custom_call" | custom-call | tf_op jit(solution)/shard_map/pallas_call | solution.py:374

commit v6 on v5

--- a/solution.py
+++ b/solution.py
@@ -196,7 +196,7 @@
     for h in range(2):
         for k in range(2):
             go(f"dy{h}{k}", "grads", db.at[1, h, part[k]], db.at[t_to, h, part[k]], y_in)
-    for d in (1, 3, 2):
+    for d in (2, 1, 3):
         go(f"dx{d}", "dx", dx.at[0, 0:GROUP], dx.at[d, 0:GROUP], x_of[d])
     out_ref[...] = x_ref[...] + preact * cdf
     blocks = [(1 - yh) * 2 + 1 - c, (1 - yh) * 2 + c, yh * 2 + 1 - c, yh * 2 + c]

time: 46.3 us -> 47.9 us (1.035)
  Pallas kernels: 45.6 us -> 47.1 us
    pallas_call x1, Pallas kernels: 44.8 us -> 46.4 us  [shards(): pl.pallas_call(body, out_shape=shapes, in_specs=[hbm] * 3, out_specs=(vme...]
where the time goes in v6:
time: 47.9 us; the launch traced here: 47.8 us
  Pallas kernels  47.1 us (98%)
  between operations  0.64 us (1%)
    pallas_call x1, Pallas kernels, shards(): pl.pallas_call(body, out_shape=shapes, in_specs=[hbm] * 3, out_specs=(vme...  46.4 us

profile of v6, /device:TPU:8, one launch (start us, length us, event | category | flops | bytes accessed | tf_op | source)
XLA Modules:
  0.0 47.8 jit_solution(17178226536275763434)
XLA Ops:
  0.6 46.4 %shard_map.58 = (f32[192,256]{1,0:T(8,128)S(1)}, f32[192,256]{1,0:T(8,128)S(1)}, f32[3,6,192]{2,1,0:T(8,128)S(1)}) custom-call(f32[192,256]{1,0:T(8,128)} %refs_0_.1, bf16[3,192,768]{2,1,0:T(8,128)(2,1)} %refs_1_.1, f32[192,256]{1,0:T(8,128)} %refs_2_.1), custom_call_target="tpu_custom_call" | custom-call | tf_op jit(solution)/shard_map/pallas_call | solution.py:339
  47.0 0.8 %shard_map.59 = (f32[192,256]{1,0:T(8,128)}, f32[192,256]{1,0:T(8,128)}, f32[3,6,192]{2,1,0:T(8,128)}) custom-call(f32[192,256]{1,0:T(8,128)S(1)} %get-tuple-element.6.refs_0_, f32[192,256]{1,0:T(8,128)S(1)} %get-tuple-element.7.refs_1_, f32[3,6,192]{2,1,0:T(8,128)S(1)} %get-tuple-element.8.refs_2_), custom_call_target="tpu_custom_call" | custom-call | tf_op jit(solution)/shard_map/pallas_call | solution.py:374
